TPU v7x, 1024 devices: a whole 4x8x16 slice. The times are simulated.
1024 devices in a mesh: len: 8 (over x, core), brick: 128 (over z, y).
Axes of the slice: x: 4, y: 8, z: 16, core: 2. Of those that a mesh axis runs over, the one named last changes fastest.
Arguments:
- forces: float32 [3, 64, 2048, 128], P(None, 'len', 'brick'), may hold values from -6 to 6
- modulus: float32 [64, 2048, 128], P('len', 'brick'), may hold values from 1 to 10
- occupancy: int32 [64, 2048, 128], P('len', 'brick'), may hold values 0 or 1
- bonded: int32 [64, 2048, 128], P('len', 'brick'), may hold values 0 or 1
Outputs:
- solution: float32 [3, 64, 2048, 128], P(None, 'len', 'brick')
All inputs are finite; a program needn't handle non-finite values. No bound on the sum of `occupancy` or of `bonded` on one device may be relied on, other than what follows from the above.
Results may differ from a plain program's by a relative error of at most 0.0001.
Values sent between devices are 32-bit elements; how exact they have to be, the bound alone decides.
A program may use at most 64 MiB of HBM per device.

v0:
```python
import jax
import jax.numpy as jnp
from jax import lax
from jax.sharding import PartitionSpec as P

LEVELS = 3
POST_SWEEPS = 2
COARSE_SWEEPS = 4


DAMPING = 0.6
COUPLING = 0.2
MASS_TERM = 0.1
PENALTY = 20.0
COARSE_SCALE = 0.25


def extended_2(block, sides, width):
    for axis, dim in sides:
        count = lax.axis_size(axis)
        forward = [(i, i + 1) for i in range(count - 1)]
        backward = [(target, source) for source, target in forward]
        low = lax.ppermute(
            lax.slice_in_dim(block, block.shape[dim] - width, None, axis=dim), axis, forward
        )
        high = lax.ppermute(lax.slice_in_dim(block, 0, width, axis=dim), axis, backward)
        block = jnp.concatenate([low, block, high], axis=dim)
    return block


def smooth(extended):
    ndims = extended.ndim
    padded = jnp.pad(extended, [(0, 0)] * (ndims - 1) + [(1, 1)])
    depth = padded.shape[-1]
    total = extended + 0.5 * (
        lax.slice_in_dim(padded, 0, depth - 2, axis=ndims - 1)
        + lax.slice_in_dim(padded, 2, depth, axis=ndims - 1)
    )
    for axis_now in (ndims - 2, ndims - 3):
        extent = total.shape[axis_now]
        total = lax.slice_in_dim(total, 1, extent - 1, axis=axis_now) + 0.5 * (
            lax.slice_in_dim(total, 0, extent - 2, axis=axis_now)
            + lax.slice_in_dim(total, 2, extent, axis=axis_now)
        )
    return total


def weights_only(coeff_ext):
    centre = coeff_ext[1:-1, 1:-1, :]
    weight_total = 6.0 * centre + smooth(coeff_ext)
    return (centre, weight_total)


def stencil(field_ext, coeff_ext):
    centre, weight_total = weights_only(coeff_ext)
    field_mid = field_ext[:, 1:-1, 1:-1, :]
    product_ext = coeff_ext[None] * field_ext
    product_mid = product_ext[:, 1:-1, 1:-1, :]
    gathered_sum = centre * (smooth(field_ext) - field_mid) + smooth(product_ext) - product_mid
    return (centre, weight_total, gathered_sum)


def apply_operator(field_ext, coeff_ext, shift_term):
    centre, weight_total, gathered_sum = stencil(field_ext, coeff_ext)
    field_mid = field_ext[:, 1:-1, 1:-1, :]
    return (
        (weight_total + shift_term) * field_mid
        - gathered_sum
        + COUPLING * centre * jnp.sum(field_mid, axis=0)
    )


def jacobi_step(field_ext, coeff_ext, shift_term, source, extra):
    centre, weight_total, gathered_sum = stencil(field_ext, coeff_ext)
    field_mid = field_ext[:, 1:-1, 1:-1, :]
    applied = (
        (weight_total + shift_term) * field_mid
        - gathered_sum
        + COUPLING * centre * jnp.sum(field_mid, axis=0)
    )
    return field_mid + DAMPING * (source - applied) / (
        weight_total + shift_term + COUPLING * centre + extra
    )


def first_step(coeff_ext, shift_term, source):
    centre, weight_total = weights_only(coeff_ext)
    return DAMPING * source / (weight_total + shift_term + COUPLING * centre)


def restrict_field(values):
    shaped = values.reshape(
        values.shape[0], values.shape[1] // 2, 2, values.shape[2] // 2, 2, values.shape[3] // 2, 2
    )
    return jnp.mean(shaped, axis=(2, 4, 6))


def restrict_cells(values):
    return restrict_field(values[None])[0]


def prolong(values):
    return jnp.repeat(jnp.repeat(jnp.repeat(values, 2, axis=1), 2, axis=2), 2, axis=3)


def grow_field(values):
    return extended_2(values, (("len", 1), ("brick", 2)), 1)


def grow_coeff(values):
    return extended_2(values, (("len", 0), ("brick", 1)), 1)


def body(forces, modulus, occupancy, bonded):
    coeffs = [modulus * occupancy.astype(jnp.float32)]
    shifts = [MASS_TERM + PENALTY * bonded.astype(jnp.float32)]
    for tier_index in range(LEVELS):
        coeffs.append(COARSE_SCALE * restrict_cells(coeffs[-1]))
        shifts.append(restrict_cells(shifts[-1]))
    first_coeff = grow_coeff(coeffs[0])
    last_tier = LEVELS
    coeff_exts = [first_coeff] + [
        grow_coeff(coeffs[tier_index]) for tier_index in range(1, last_tier)
    ]

    def coarsest_solve(source):
        coeff_ext = grow_coeff(coeffs[LEVELS])
        shift_term = shifts[LEVELS]
        iterate = first_step(coeff_ext, shift_term, source)
        for repeat_idx in range(COARSE_SWEEPS - 1):
            iterate = jacobi_step(grow_field(iterate), coeff_ext, shift_term, source, 0.0)
        return iterate

    def multigrid_pass(tier_index, source):
        coeff_ext = coeff_exts[tier_index]
        shift_term = shifts[tier_index]
        iterate = first_step(coeff_ext, shift_term, source)
        iterate = jacobi_step(grow_field(iterate), coeff_ext, shift_term, source, 0.0)
        residual = source - apply_operator(grow_field(iterate), coeff_ext, shift_term)
        coarse_source = restrict_field(residual)
        if tier_index + 1 == LEVELS:
            correction = coarsest_solve(coarse_source)
        else:
            correction = multigrid_pass(tier_index + 1, coarse_source)
        iterate = iterate + prolong(correction)
        for repeat_idx in range(POST_SWEEPS):
            iterate = jacobi_step(grow_field(iterate), coeff_ext, shift_term, source, 0.0)
        return iterate

    return multigrid_pass(0, forces)


def solution(mesh):
    in_specs = (
        P(None, "len", "brick", None),
        P("len", "brick", None),
        P("len", "brick", None),
        P("len", "brick", None),
    )
    out_specs = P(None, "len", "brick", None)
    return jax.shard_map(body, mesh=mesh, in_specs=in_specs, out_specs=out_specs, check_vma=False)
```

profile of v0, /device:TPU:774, one launch (start us, length us, event | category | flops | bytes accessed | tf_op | source)
XLA Modules:
  0.0 382.5 jit_solution(8324277399174935719)
XLA Ops:
  0.9 5.6 %reshape_broadcast_in_dim.8 = f32[4,2,8,2,64,2]{5,4,3,2,1,0:T(8,128)} reshape(f32[8,16,128]{2,1,0:T(8,128)S(1)} %convert_multiply_fusion) | data formatting | bytes 131072 | tf_op jit(solution)/shard_map/reshape;broadcast_in_dim | solution.py:92
  6.5 2.6 reduce_sum.240
  14.1 3.4 collective-permute-start.1
  19.5 6.6 %collective-permute-start.27 = (f32[4,1,32]{2,1,0:T(1,128)S(1)}, f32[4,1,32]{2,1,0:T(1,128)S(1)}, u32[]{:S(2)}, u32[]{:S(2)}) collective-permute-start(f32[4,1,32]{2,1,0:T(1,128)S(1)} %get-tuple-element.136), channel_id=1, source_target_pairs={{1,0},{2,1},{3,2},{4,3},{5,4},{6,5},{7,6},{8,7},{9,8},{10,9},{11,1... | collective-permute-start | bytes 1544 | tf_op jit(solution)/shard_map/ppermute | solution.py:26
  28.0 3.4 collective-permute-start.13
  36.3 7.0 %collective-permute-start.15 = (f32[6,1,64]{2,1,0:T(1,128)S(1)}, f32[6,1,64]{2,1,0:T(1,128)S(1)}, u32[]{:S(2)}, u32[]{:S(2)}) collective-permute-start(f32[6,1,64]{2,1,0:T(1,128)S(1)} %get-tuple-element.111), channel_id=1, source_target_pairs={{1,0},{2,1},{3,2},{4,3},{5,4},{6,5},{7,6},{8,7},{9,8},{10,9},{11,1... | collective-permute-start | bytes 4616 | tf_op jit(solution)/shard_map/ppermute | solution.py:26
  45.2 6.9 %collective-permute-done.14 = f32[6,1,64]{2,1,0:T(1,128)S(1)} collective-permute-done((f32[6,1,64]{2,1,0:T(1,128)S(1)}, f32[6,1,64]{2,1,0:T(1,128)S(1)}, u32[]{:S(2)}, u32[]{:S(2)}) %collective-permute-start.14) | collective-permute-done | bytes 1568 | tf_op jit(solution)/shard_map/ppermute | solution.py:23
  54.2 3.9 %collective-permute-start.2 = (f32[10,1,128]{2,1,0:T(1,128)S(1)}, f32[10,1,128]{2,1,0:T(1,128)S(1)}, u32[]{:S(2)}, u32[]{:S(2)}) collective-permute-start(f32[10,1,128]{2,1,0:T(1,128)S(1)} %get-tuple-element.71), channel_id=1, source_target_pairs={{0,1},{1,2},{2,3},{3,4},{4,5},{5,6},{6,7},{7,8},{8,9},{9,10},{10,1... | collective-permute-start | bytes 15368 | tf_op jit(solution)/shard_map/ppermute | solution.py:23
  58.1 4.9 %collective-permute-done.2 = f32[10,1,128]{2,1,0:T(1,128)S(1)} collective-permute-done((f32[10,1,128]{2,1,0:T(1,128)S(1)}, f32[10,1,128]{2,1,0:T(1,128)S(1)}, u32[]{:S(2)}, u32[]{:S(2)}) %collective-permute-start.2) | collective-permute-done | bytes 5152 | tf_op jit(solution)/shard_map/ppermute | solution.py:23
  63.3 5.6 %reshape_broadcast_in_dim.9 = f32[4,2,8,2,64,2]{5,4,3,2,1,0:T(8,128)} reshape(f32[8,16,128]{2,1,0:T(8,128)S(1)} %get-tuple-element.83) | data formatting | bytes 131072 | tf_op jit(solution)/shard_map/reshape;broadcast_in_dim | solution.py:92
  68.8 2.5 reduce_sum.241
  76.7 3.2 collective-permute-start.5
  82.0 3.0 collective-permute-done.4
  86.9 3.9 %collective-permute-start.6 = (f32[3,10,1,128]{3,2,1,0:T(1,128)S(1)}, f32[3,10,1,128]{3,2,1,0:T(1,128)S(1)}, u32[]{:S(2)}, u32[]{:S(2)}) collective-permute-start(f32[3,10,1,128]{3,2,1,0:T(1,128)S(1)} %get-tuple-element.53), channel_id=1, source_target_pairs={{0,1},{1,2},{2,3},{3,4},{4,5},{5,6},{6,7},{7,8},{8,9},{9,10},{10,1... | collective-permute-start | bytes 46088 | tf_op jit(solution)/shard_map/ppermute | solution.py:23
  90.9 5.0 %collective-permute-done.6 = f32[3,10,1,128]{3,2,1,0:T(1,128)S(1)} collective-permute-done((f32[3,10,1,128]{3,2,1,0:T(1,128)S(1)}, f32[3,10,1,128]{3,2,1,0:T(1,128)S(1)}, u32[]{:S(2)}, u32[]{:S(2)}) %collective-permute-start.6) | collective-permute-done | bytes 15392 | tf_op jit(solution)/shard_map/ppermute | solution.py:23
  98.7 2.4 collective-permute-start.8
  103.0 3.9 %collective-permute-start.38 = (f32[3,1,16]{2,1,0:T(1,128)S(1)}, f32[3,1,16]{2,1,0:T(1,128)S(1)}, u32[]{:S(2)}, u32[]{:S(2)}) collective-permute-start(f32[3,1,16]{2,1,0:T(1,128)S(1)} %get-tuple-element.141), channel_id=1, source_target_pairs={{0,1},{1,2},{2,3},{3,4},{4,5},{5,6},{6,7},{7,8},{8,9},{9,10},{10,1... | collective-permute-start | bytes 584 | tf_op jit(solution)/shard_map/ppermute | solution.py:23
  107.0 5.2 %collective-permute-start.11 = (f32[3,10,1,128]{3,2,1,0:T(1,128)S(1)}, f32[3,10,1,128]{3,2,1,0:T(1,128)S(1)}, u32[]{:S(2)}, u32[]{:S(2)}) collective-permute-start(f32[3,10,1,128]{3,2,1,0:T(1,128)S(1)} %get-tuple-element.52), channel_id=1, source_target_pairs={{1,0},{2,1},{3,2},{4,3},{5,4},{6,5},{7,6},{8,7},{9,8},{10,9},{11,1... | collective-permute-start | bytes 46088 | tf_op jit(solution)/shard_map/ppermute | solution.py:26
  114.2 7.0 %collective-permute-done.10 = f32[3,10,1,128]{3,2,1,0:T(1,128)S(1)} collective-permute-done((f32[3,10,1,128]{3,2,1,0:T(1,128)S(1)}, f32[3,10,1,128]{3,2,1,0:T(1,128)S(1)}, u32[]{:S(2)}, u32[]{:S(2)}) %collective-permute-start.10) | collective-permute-done | bytes 15392 | tf_op jit(solution)/shard_map/ppermute | solution.py:23
  122.1 14.0 %reshape.274 = f32[3,4,2,8,2,64,2]{6,5,4,3,2,1,0:T(8,128)} reshape(f32[3,8,16,128]{3,2,1,0:T(8,128)S(1)} %fusion.68) | data formatting | bytes 393216 | tf_op jit(solution)/shard_map/reshape | solution.py:92
  136.1 5.5 %reduce_sum.239 = f32[3,4,8,64]{3,2,1,0:T(8,128)S(1)} reduce(f32[3,4,2,8,2,64,2]{6,5,4,3,2,1,0:T(8,128)} %reshape.274, f32[]{:T(128)} %constant.46.clone.1), dimensions={2,4,6}, to_apply=%region_2.0 | reduce | flops 43008 | bytes 221188 | tf_op jit(solution)/shard_map/reduce_sum | solution.py:95
  146.0 2.6 collective-permute-done.16
  150.5 3.9 %collective-permute-start.18 = (f32[3,6,1,64]{3,2,1,0:T(1,128)S(1)}, f32[3,6,1,64]{3,2,1,0:T(1,128)S(1)}, u32[]{:S(2)}, u32[]{:S(2)}) collective-permute-start(f32[3,6,1,64]{3,2,1,0:T(1,128)S(1)} %get-tuple-element.79), channel_id=1, source_target_pairs={{0,1},{1,2},{2,3},{3,4},{4,5},{5,6},{6,7},{7,8},{8,9},{9,10},{10,1... | collective-permute-start | bytes 13832 | tf_op jit(solution)/shard_map/ppermute | solution.py:23
  154.5 4.9 %collective-permute-done.18 = f32[3,6,1,64]{3,2,1,0:T(1,128)S(1)} collective-permute-done((f32[3,6,1,64]{3,2,1,0:T(1,128)S(1)}, f32[3,6,1,64]{3,2,1,0:T(1,128)S(1)}, u32[]{:S(2)}, u32[]{:S(2)}) %collective-permute-start.18) | collective-permute-done | bytes 4640 | tf_op jit(solution)/shard_map/ppermute | solution.py:23
  164.3 2.5 collective-permute-done.20
  168.7 4.1 %collective-permute-start.22 = (f32[3,6,1,64]{3,2,1,0:T(1,128)S(1)}, f32[3,6,1,64]{3,2,1,0:T(1,128)S(1)}, u32[]{:S(2)}, u32[]{:S(2)}) collective-permute-start(f32[3,6,1,64]{3,2,1,0:T(1,128)S(1)} %get-tuple-element.77), channel_id=1, source_target_pairs={{0,1},{1,2},{2,3},{3,4},{4,5},{5,6},{6,7},{7,8},{8,9},{9,10},{10,1... | collective-permute-start | bytes 13832 | tf_op jit(solution)/shard_map/ppermute | solution.py:23
  172.9 4.7 %collective-permute-done.22 = f32[3,6,1,64]{3,2,1,0:T(1,128)S(1)} collective-permute-done((f32[3,6,1,64]{3,2,1,0:T(1,128)S(1)}, f32[3,6,1,64]{3,2,1,0:T(1,128)S(1)}, u32[]{:S(2)}, u32[]{:S(2)}) %collective-permute-start.22) | collective-permute-done | bytes 4640 | tf_op jit(solution)/shard_map/ppermute | solution.py:23
  184.3 2.5 collective-permute-done.28
  188.7 3.9 %collective-permute-start.30 = (f32[3,4,1,32]{3,2,1,0:T(1,128)S(1)}, f32[3,4,1,32]{3,2,1,0:T(1,128)S(1)}, u32[]{:S(2)}, u32[]{:S(2)}) collective-permute-start(f32[3,4,1,32]{3,2,1,0:T(1,128)S(1)} %get-tuple-element.108), channel_id=1, source_target_pairs={{0,1},{1,2},{2,3},{3,4},{4,5},{5,6},{6,7},{7,8},{8,9},{9,10},{10,1... | collective-permute-start | bytes 4616 | tf_op jit(solution)/shard_map/ppermute | solution.py:23
  192.7 4.9 %collective-permute-done.30 = f32[3,4,1,32]{3,2,1,0:T(1,128)S(1)} collective-permute-done((f32[3,4,1,32]{3,2,1,0:T(1,128)S(1)}, f32[3,4,1,32]{3,2,1,0:T(1,128)S(1)}, u32[]{:S(2)}, u32[]{:S(2)}) %collective-permute-start.30) | collective-permute-done | bytes 1568 | tf_op jit(solution)/shard_map/ppermute | solution.py:23
  202.3 2.5 collective-permute-done.32
  206.7 3.9 %collective-permute-start.34 = (f32[3,4,1,32]{3,2,1,0:T(1,128)S(1)}, f32[3,4,1,32]{3,2,1,0:T(1,128)S(1)}, u32[]{:S(2)}, u32[]{:S(2)}) collective-permute-start(f32[3,4,1,32]{3,2,1,0:T(1,128)S(1)} %get-tuple-element.106), channel_id=1, source_target_pairs={{0,1},{1,2},{2,3},{3,4},{4,5},{5,6},{6,7},{7,8},{8,9},{9,10},{10,1... | collective-permute-start | bytes 4616 | tf_op jit(solution)/shard_map/ppermute | solution.py:23
  210.7 4.9 %collective-permute-done.34 = f32[3,4,1,32]{3,2,1,0:T(1,128)S(1)} collective-permute-done((f32[3,4,1,32]{3,2,1,0:T(1,128)S(1)}, f32[3,4,1,32]{3,2,1,0:T(1,128)S(1)}, u32[]{:S(2)}, u32[]{:S(2)}) %collective-permute-start.34) | collective-permute-done | bytes 1568 | tf_op jit(solution)/shard_map/ppermute | solution.py:23
  220.5 2.5 collective-permute-done.40
  224.9 3.9 %collective-permute-start.42 = (f32[3,3,1,16]{3,2,0,1:T(1,128)S(1)}, f32[3,3,1,16]{3,2,0,1:T(1,128)S(1)}, u32[]{:S(2)}, u32[]{:S(2)}) collective-permute-start(f32[3,3,1,16]{3,2,0,1:T(1,128)S(1)} %get-tuple-element.133), channel_id=1, source_target_pairs={{0,1},{1,2},{2,3},{3,4},{4,5},{5,6},{6,7},{7,8},{8,9},{9,10},{10,1... | collective-permute-start | bytes 1736 | tf_op jit(solution)/shard_map/ppermute | solution.py:23
  228.9 4.9 %collective-permute-done.42 = f32[3,3,1,16]{3,2,0,1:T(1,128)S(1)} collective-permute-done((f32[3,3,1,16]{3,2,0,1:T(1,128)S(1)}, f32[3,3,1,16]{3,2,0,1:T(1,128)S(1)}, u32[]{:S(2)}, u32[]{:S(2)}) %collective-permute-start.42) | collective-permute-done | bytes 608 | tf_op jit(solution)/shard_map/ppermute | solution.py:23
  238.4 2.5 collective-permute-done.44
  242.8 3.9 %collective-permute-start.46 = (f32[3,3,1,16]{3,2,0,1:T(1,128)S(1)}, f32[3,3,1,16]{3,2,0,1:T(1,128)S(1)}, u32[]{:S(2)}, u32[]{:S(2)}) collective-permute-start(f32[3,3,1,16]{3,2,0,1:T(1,128)S(1)} %get-tuple-element.131), channel_id=1, source_target_pairs={{0,1},{1,2},{2,3},{3,4},{4,5},{5,6},{6,7},{7,8},{8,9},{9,10},{10,1... | collective-permute-start | bytes 1736 | tf_op jit(solution)/shard_map/ppermute | solution.py:23
  246.8 4.9 %collective-permute-done.46 = f32[3,3,1,16]{3,2,0,1:T(1,128)S(1)} collective-permute-done((f32[3,3,1,16]{3,2,0,1:T(1,128)S(1)}, f32[3,3,1,16]{3,2,0,1:T(1,128)S(1)}, u32[]{:S(2)}, u32[]{:S(2)}) %collective-permute-start.46) | collective-permute-done | bytes 608 | tf_op jit(solution)/shard_map/ppermute | solution.py:23
  256.3 2.5 collective-permute-done.48
  260.7 3.9 %collective-permute-start.50 = (f32[3,3,1,16]{3,2,0,1:T(1,128)S(1)}, f32[3,3,1,16]{3,2,0,1:T(1,128)S(1)}, u32[]{:S(2)}, u32[]{:S(2)}) collective-permute-start(f32[3,3,1,16]{3,2,0,1:T(1,128)S(1)} %get-tuple-element.129), channel_id=1, source_target_pairs={{0,1},{1,2},{2,3},{3,4},{4,5},{5,6},{6,7},{7,8},{8,9},{9,10},{10,1... | collective-permute-start | bytes 1736 | tf_op jit(solution)/shard_map/ppermute | solution.py:23
  264.7 4.9 %collective-permute-done.50 = f32[3,3,1,16]{3,2,0,1:T(1,128)S(1)} collective-permute-done((f32[3,3,1,16]{3,2,0,1:T(1,128)S(1)}, f32[3,3,1,16]{3,2,0,1:T(1,128)S(1)}, u32[]{:S(2)}, u32[]{:S(2)}) %collective-permute-start.50) | collective-permute-done | bytes 608 | tf_op jit(solution)/shard_map/ppermute | solution.py:23
  274.4 2.5 collective-permute-done.52
  278.9 3.9 %collective-permute-start.54 = (f32[3,4,1,32]{3,2,1,0:T(1,128)S(1)}, f32[3,4,1,32]{3,2,1,0:T(1,128)S(1)}, u32[]{:S(2)}, u32[]{:S(2)}) collective-permute-start(f32[3,4,1,32]{3,2,1,0:T(1,128)S(1)} %get-tuple-element.104), channel_id=1, source_target_pairs={{0,1},{1,2},{2,3},{3,4},{4,5},{5,6},{6,7},{7,8},{8,9},{9,10},{10,1... | collective-permute-start | bytes 4616 | tf_op jit(solution)/shard_map/ppermute | solution.py:23
  282.9 4.9 %collective-permute-done.54 = f32[3,4,1,32]{3,2,1,0:T(1,128)S(1)} collective-permute-done((f32[3,4,1,32]{3,2,1,0:T(1,128)S(1)}, f32[3,4,1,32]{3,2,1,0:T(1,128)S(1)}, u32[]{:S(2)}, u32[]{:S(2)}) %collective-permute-start.54) | collective-permute-done | bytes 1568 | tf_op jit(solution)/shard_map/ppermute | solution.py:23
  292.4 2.5 collective-permute-done.56
  296.9 3.9 %collective-permute-start.58 = (f32[3,4,1,32]{3,2,1,0:T(1,128)S(1)}, f32[3,4,1,32]{3,2,1,0:T(1,128)S(1)}, u32[]{:S(2)}, u32[]{:S(2)}) collective-permute-start(f32[3,4,1,32]{3,2,1,0:T(1,128)S(1)} %get-tuple-element.102), channel_id=1, source_target_pairs={{0,1},{1,2},{2,3},{3,4},{4,5},{5,6},{6,7},{7,8},{8,9},{9,10},{10,1... | collective-permute-start | bytes 4616 | tf_op jit(solution)/shard_map/ppermute | solution.py:23
  300.8 4.9 %collective-permute-done.58 = f32[3,4,1,32]{3,2,1,0:T(1,128)S(1)} collective-permute-done((f32[3,4,1,32]{3,2,1,0:T(1,128)S(1)}, f32[3,4,1,32]{3,2,1,0:T(1,128)S(1)}, u32[]{:S(2)}, u32[]{:S(2)}) %collective-permute-start.58) | collective-permute-done | bytes 1568 | tf_op jit(solution)/shard_map/ppermute | solution.py:23
  308.5 2.4 collective-permute-start.60
  310.9 2.6 collective-permute-done.60
  315.4 3.9 %collective-permute-start.62 = (f32[3,6,1,64]{3,2,1,0:T(1,128)S(1)}, f32[3,6,1,64]{3,2,1,0:T(1,128)S(1)}, u32[]{:S(2)}, u32[]{:S(2)}) collective-permute-start(f32[3,6,1,64]{3,2,1,0:T(1,128)S(1)} %get-tuple-element.75), channel_id=1, source_target_pairs={{0,1},{1,2},{2,3},{3,4},{4,5},{5,6},{6,7},{7,8},{8,9},{9,10},{10,1... | collective-permute-start | bytes 13832 | tf_op jit(solution)/shard_map/ppermute | solution.py:23
  319.4 4.9 %collective-permute-done.62 = f32[3,6,1,64]{3,2,1,0:T(1,128)S(1)} collective-permute-done((f32[3,6,1,64]{3,2,1,0:T(1,128)S(1)}, f32[3,6,1,64]{3,2,1,0:T(1,128)S(1)}, u32[]{:S(2)}, u32[]{:S(2)}) %collective-permute-start.62) | collective-permute-done | bytes 4640 | tf_op jit(solution)/shard_map/ppermute | solution.py:23
  326.7 2.4 collective-permute-start.64
  329.1 2.6 collective-permute-done.64
  333.7 3.9 %collective-permute-start.66 = (f32[3,6,1,64]{3,2,1,0:T(1,128)S(1)}, f32[3,6,1,64]{3,2,1,0:T(1,128)S(1)}, u32[]{:S(2)}, u32[]{:S(2)}) collective-permute-start(f32[3,6,1,64]{3,2,1,0:T(1,128)S(1)} %get-tuple-element.73), channel_id=1, source_target_pairs={{0,1},{1,2},{2,3},{3,4},{4,5},{5,6},{6,7},{7,8},{8,9},{9,10},{10,1... | collective-permute-start | bytes 13832 | tf_op jit(solution)/shard_map/ppermute | solution.py:23
  337.6 4.9 %collective-permute-done.66 = f32[3,6,1,64]{3,2,1,0:T(1,128)S(1)} collective-permute-done((f32[3,6,1,64]{3,2,1,0:T(1,128)S(1)}, f32[3,6,1,64]{3,2,1,0:T(1,128)S(1)}, u32[]{:S(2)}, u32[]{:S(2)}) %collective-permute-start.66) | collective-permute-done | bytes 4640 | tf_op jit(solution)/shard_map/ppermute | solution.py:23
  346.0 2.4 collective-permute-start.68
  348.4 2.7 collective-permute-done.68
  353.1 3.9 %collective-permute-start.70 = (f32[3,10,1,128]{3,2,1,0:T(1,128)S(1)}, f32[3,10,1,128]{3,2,1,0:T(1,128)S(1)}, u32[]{:S(2)}, u32[]{:S(2)}) collective-permute-start(f32[3,10,1,128]{3,2,1,0:T(1,128)S(1)} %get-tuple-element.49), channel_id=1, source_target_pairs={{0,1},{1,2},{2,3},{3,4},{4,5},{5,6},{6,7},{7,8},{8,9},{9,10},{10,1... | collective-permute-start | bytes 46088 | tf_op jit(solution)/shard_map/ppermute | solution.py:23
  357.0 5.0 %collective-permute-done.70 = f32[3,10,1,128]{3,2,1,0:T(1,128)S(1)} collective-permute-done((f32[3,10,1,128]{3,2,1,0:T(1,128)S(1)}, f32[3,10,1,128]{3,2,1,0:T(1,128)S(1)}, u32[]{:S(2)}, u32[]{:S(2)}) %collective-permute-start.70) | collective-permute-done | bytes 15392 | tf_op jit(solution)/shard_map/ppermute | solution.py:23
  364.9 2.4 collective-permute-start.72
  367.3 2.7 collective-permute-done.72
  372.0 3.9 %collective-permute-start.74 = (f32[3,10,1,128]{3,2,1,0:T(1,128)S(1)}, f32[3,10,1,128]{3,2,1,0:T(1,128)S(1)}, u32[]{:S(2)}, u32[]{:S(2)}) collective-permute-start(f32[3,10,1,128]{3,2,1,0:T(1,128)S(1)} %get-tuple-element.47), channel_id=1, source_target_pairs={{0,1},{1,2},{2,3},{3,4},{4,5},{5,6},{6,7},{7,8},{8,9},{9,10},{10,1... | collective-permute-start | bytes 46088 | tf_op jit(solution)/shard_map/ppermute | solution.py:23
  375.9 5.0 %collective-permute-done.74 = f32[3,10,1,128]{3,2,1,0:T(1,128)S(1)} collective-permute-done((f32[3,10,1,128]{3,2,1,0:T(1,128)S(1)}, f32[3,10,1,128]{3,2,1,0:T(1,128)S(1)}, u32[]{:S(2)}, u32[]{:S(2)}) %collective-permute-start.74) | collective-permute-done | bytes 15392 | tf_op jit(solution)/shard_map/ppermute | solution.py:23
  (295 shorter events, 117.4 us)
Async XLA Ops:
  9.7 9.7 %collective-permute-start.25 = (f32[1,4,32]{2,1,0:T(4,128)S(1)}, f32[1,4,32]{2,1,0:T(4,128)S(1)}, u32[]{:S(2)}, u32[]{:S(2)}) collective-permute-start(f32[1,4,32]{2,1,0:T(4,128)S(1)} %get-tuple-element.140), channel_id=1, source_target_pairs={{128,0},{256,128},{384,256},{512,384},{640,512},{768,640},{896,768... | collective-permute-start | bytes 1544 | tf_op jit(solution)/shard_map/ppermute | solution.py:26
  11.9 7.5 %collective-permute-start.24 = (f32[1,4,32]{2,1,0:T(4,128)S(1)}, f32[1,4,32]{2,1,0:T(4,128)S(1)}, u32[]{:S(2)}, u32[]{:S(2)}) collective-permute-start(f32[1,4,32]{2,1,0:T(4,128)S(1)} %get-tuple-element.139), channel_id=1, source_target_pairs={{0,128},{128,256},{256,384},{384,512},{512,640},{640,768},{768,896... | collective-permute-start | bytes 1544 | tf_op jit(solution)/shard_map/ppermute | solution.py:23
  14.1 38.1 %collective-permute-start.1 = (f32[1,16,128]{2,1,0:T(8,128)S(1)}, f32[1,16,128]{2,1,0:T(8,128)S(1)}, u32[]{:S(2)}, u32[]{:S(2)}) collective-permute-start(f32[1,16,128]{2,1,0:T(8,128)S(1)} %get-tuple-element.85), channel_id=1, source_target_pairs={{128,0},{256,128},{384,256},{512,384},{640,512},{768,640},{896,768... | collective-permute-start | bytes 24584 | tf_op jit(solution)/shard_map/ppermute | solution.py:26
  17.5 34.7 %collective-permute-start = (f32[1,16,128]{2,1,0:T(8,128)S(1)}, f32[1,16,128]{2,1,0:T(8,128)S(1)}, u32[]{:S(2)}, u32[]{:S(2)}) collective-permute-start(f32[1,16,128]{2,1,0:T(8,128)S(1)} %get-tuple-element.84), channel_id=1, source_target_pairs={{0,128},{128,256},{256,384},{384,512},{512,640},{640,768},{768,896... | collective-permute-start | bytes 24584 | tf_op jit(solution)/shard_map/ppermute | solution.py:23
  19.5 11.9 %collective-permute-start.27 = (f32[4,1,32]{2,1,0:T(1,128)S(1)}, f32[4,1,32]{2,1,0:T(1,128)S(1)}, u32[]{:S(2)}, u32[]{:S(2)}) collective-permute-start(f32[4,1,32]{2,1,0:T(1,128)S(1)} %get-tuple-element.136), channel_id=1, source_target_pairs={{1,0},{2,1},{3,2},{4,3},{5,4},{6,5},{7,6},{8,7},{9,8},{10,9},{11,1... | collective-permute-start | bytes 1544 | tf_op jit(solution)/shard_map/ppermute | solution.py:26
  26.1 8.8 %collective-permute-start.26 = (f32[4,1,32]{2,1,0:T(1,128)S(1)}, f32[4,1,32]{2,1,0:T(1,128)S(1)}, u32[]{:S(2)}, u32[]{:S(2)}) collective-permute-start(f32[4,1,32]{2,1,0:T(1,128)S(1)} %get-tuple-element.135), channel_id=1, source_target_pairs={{0,1},{1,2},{2,3},{3,4},{4,5},{5,6},{6,7},{7,8},{8,9},{9,10},{10,1... | collective-permute-start | bytes 1544 | tf_op jit(solution)/shard_map/ppermute | solution.py:23
  28.0 7.0 %collective-permute-start.13 = (f32[1,8,64]{2,1,0:T(8,128)S(1)}, f32[1,8,64]{2,1,0:T(8,128)S(1)}, u32[]{:S(2)}, u32[]{:S(2)}) collective-permute-start(f32[1,8,64]{2,1,0:T(8,128)S(1)} %get-tuple-element.120), channel_id=1, source_target_pairs={{128,0},{256,128},{384,256},{512,384},{640,512},{768,640},{896,768... | collective-permute-start | bytes 6152 | tf_op jit(solution)/shard_map/ppermute | solution.py:26
  31.4 4.9 %collective-permute-start.12 = (f32[1,8,64]{2,1,0:T(8,128)S(1)}, f32[1,8,64]{2,1,0:T(8,128)S(1)}, u32[]{:S(2)}, u32[]{:S(2)}) collective-permute-start(f32[1,8,64]{2,1,0:T(8,128)S(1)} %get-tuple-element.119), channel_id=1, source_target_pairs={{0,128},{128,256},{256,384},{384,512},{512,640},{640,768},{768,896... | collective-permute-start | bytes 6152 | tf_op jit(solution)/shard_map/ppermute | solution.py:23
  36.3 8.9 %collective-permute-start.15 = (f32[6,1,64]{2,1,0:T(1,128)S(1)}, f32[6,1,64]{2,1,0:T(1,128)S(1)}, u32[]{:S(2)}, u32[]{:S(2)}) collective-permute-start(f32[6,1,64]{2,1,0:T(1,128)S(1)} %get-tuple-element.111), channel_id=1, source_target_pairs={{1,0},{2,1},{3,2},{4,3},{5,4},{6,5},{7,6},{8,7},{9,8},{10,9},{11,1... | collective-permute-start | bytes 4616 | tf_op jit(solution)/shard_map/ppermute | solution.py:26
  43.3 8.8 %collective-permute-start.14 = (f32[6,1,64]{2,1,0:T(1,128)S(1)}, f32[6,1,64]{2,1,0:T(1,128)S(1)}, u32[]{:S(2)}, u32[]{:S(2)}) collective-permute-start(f32[6,1,64]{2,1,0:T(1,128)S(1)} %get-tuple-element.110), channel_id=1, source_target_pairs={{0,1},{1,2},{2,3},{3,4},{4,5},{5,6},{6,7},{7,8},{8,9},{9,10},{10,1... | collective-permute-start | bytes 4616 | tf_op jit(solution)/shard_map/ppermute | solution.py:23
  52.3 5.9 %collective-permute-start.3 = (f32[10,1,128]{2,1,0:T(1,128)S(1)}, f32[10,1,128]{2,1,0:T(1,128)S(1)}, u32[]{:S(2)}, u32[]{:S(2)}) collective-permute-start(f32[10,1,128]{2,1,0:T(1,128)S(1)} %get-tuple-element.72), channel_id=1, source_target_pairs={{1,0},{2,1},{3,2},{4,3},{5,4},{6,5},{7,6},{8,7},{9,8},{10,9},{11,1... | collective-permute-start | bytes 15368 | tf_op jit(solution)/shard_map/ppermute | solution.py:26
  54.2 8.8 %collective-permute-start.2 = (f32[10,1,128]{2,1,0:T(1,128)S(1)}, f32[10,1,128]{2,1,0:T(1,128)S(1)}, u32[]{:S(2)}, u32[]{:S(2)}) collective-permute-start(f32[10,1,128]{2,1,0:T(1,128)S(1)} %get-tuple-element.71), channel_id=1, source_target_pairs={{0,1},{1,2},{2,3},{3,4},{4,5},{5,6},{6,7},{7,8},{8,9},{9,10},{10,1... | collective-permute-start | bytes 15368 | tf_op jit(solution)/shard_map/ppermute | solution.py:23
  72.3 18.6 %collective-permute-start.37 = (f32[1,2,16]{2,1,0:T(2,128)S(1)}, f32[1,2,16]{2,1,0:T(2,128)S(1)}, u32[]{:S(2)}, u32[]{:S(2)}) collective-permute-start(f32[1,2,16]{2,1,0:T(2,128)S(1)} %fusion.285), channel_id=1, source_target_pairs={{128,0},{256,128},{384,256},{512,384},{640,512},{768,640},{896,768... | collective-permute-start | bytes 392 | tf_op jit(solution)/shard_map/ppermute | solution.py:26
  74.2 16.7 %collective-permute-start.36 = (f32[1,2,16]{2,1,0:T(2,128)S(1)}, f32[1,2,16]{2,1,0:T(2,128)S(1)}, u32[]{:S(2)}, u32[]{:S(2)}) collective-permute-start(f32[1,2,16]{2,1,0:T(2,128)S(1)} %fusion.285), channel_id=1, source_target_pairs={{0,128},{128,256},{256,384},{384,512},{512,640},{640,768},{768,896... | collective-permute-start | bytes 392 | tf_op jit(solution)/shard_map/ppermute | solution.py:23
  76.7 5.3 %collective-permute-start.5 = (f32[3,1,16,128]{3,2,1,0:T(8,128)S(1)}, f32[3,1,16,128]{3,2,1,0:T(8,128)S(1)}, u32[]{:S(2)}, u32[]{:S(2)}) collective-permute-start(f32[3,1,16,128]{3,2,1,0:T(8,128)S(1)} %get-tuple-element.62), channel_id=1, source_target_pairs={{128,0},{256,128},{384,256},{512,384},{640,512},{768,640},{896,768... | collective-permute-start | bytes 73736 | tf_op jit(solution)/shard_map/ppermute | solution.py:26
  79.8 5.1 %collective-permute-start.4 = (f32[3,1,16,128]{3,2,1,0:T(8,128)S(1)}, f32[3,1,16,128]{3,2,1,0:T(8,128)S(1)}, u32[]{:S(2)}, u32[]{:S(2)}) collective-permute-start(f32[3,1,16,128]{3,2,1,0:T(8,128)S(1)} %get-tuple-element.61), channel_id=1, source_target_pairs={{0,128},{128,256},{256,384},{384,512},{512,640},{640,768},{768,896... | collective-permute-start | bytes 73736 | tf_op jit(solution)/shard_map/ppermute | solution.py:23
  85.0 5.9 %collective-permute-start.7 = (f32[3,10,1,128]{3,2,1,0:T(1,128)S(1)}, f32[3,10,1,128]{3,2,1,0:T(1,128)S(1)}, u32[]{:S(2)}, u32[]{:S(2)}) collective-permute-start(f32[3,10,1,128]{3,2,1,0:T(1,128)S(1)} %get-tuple-element.54), channel_id=1, source_target_pairs={{1,0},{2,1},{3,2},{4,3},{5,4},{6,5},{7,6},{8,7},{9,8},{10,9},{11,1... | collective-permute-start | bytes 46088 | tf_op jit(solution)/shard_map/ppermute | solution.py:26
  86.9 8.9 %collective-permute-start.6 = (f32[3,10,1,128]{3,2,1,0:T(1,128)S(1)}, f32[3,10,1,128]{3,2,1,0:T(1,128)S(1)}, u32[]{:S(2)}, u32[]{:S(2)}) collective-permute-start(f32[3,10,1,128]{3,2,1,0:T(1,128)S(1)} %get-tuple-element.53), channel_id=1, source_target_pairs={{0,1},{1,2},{2,3},{3,4},{4,5},{5,6},{6,7},{7,8},{8,9},{9,10},{10,1... | collective-permute-start | bytes 46088 | tf_op jit(solution)/shard_map/ppermute | solution.py:23
  96.7 10.2 %collective-permute-start.9 = (f32[3,1,16,128]{3,2,1,0:T(8,128)S(1)}, f32[3,1,16,128]{3,2,1,0:T(8,128)S(1)}, u32[]{:S(2)}, u32[]{:S(2)}) collective-permute-start(f32[3,1,16,128]{3,2,1,0:T(8,128)S(1)} %get-tuple-element.60), channel_id=1, source_target_pairs={{128,0},{256,128},{384,256},{512,384},{640,512},{768,640},{896,768... | collective-permute-start | bytes 73736 | tf_op jit(solution)/shard_map/ppermute | solution.py:26
  98.7 8.3 %collective-permute-start.8 = (f32[3,1,16,128]{3,2,1,0:T(8,128)S(1)}, f32[3,1,16,128]{3,2,1,0:T(8,128)S(1)}, u32[]{:S(2)}, u32[]{:S(2)}) collective-permute-start(f32[3,1,16,128]{3,2,1,0:T(8,128)S(1)} %get-tuple-element.59), channel_id=1, source_target_pairs={{0,128},{128,256},{256,384},{384,512},{512,640},{640,768},{768,896... | collective-permute-start | bytes 73736 | tf_op jit(solution)/shard_map/ppermute | solution.py:23
  101.1 44.9 %collective-permute-start.39 = (f32[3,1,16]{2,1,0:T(1,128)S(1)}, f32[3,1,16]{2,1,0:T(1,128)S(1)}, u32[]{:S(2)}, u32[]{:S(2)}) collective-permute-start(f32[3,1,16]{2,1,0:T(1,128)S(1)} %get-tuple-element.142), channel_id=1, source_target_pairs={{1,0},{2,1},{3,2},{4,3},{5,4},{6,5},{7,6},{8,7},{9,8},{10,9},{11,1... | collective-permute-start | bytes 584 | tf_op jit(solution)/shard_map/ppermute | solution.py:26
  103.0 43.0 %collective-permute-start.38 = (f32[3,1,16]{2,1,0:T(1,128)S(1)}, f32[3,1,16]{2,1,0:T(1,128)S(1)}, u32[]{:S(2)}, u32[]{:S(2)}) collective-permute-start(f32[3,1,16]{2,1,0:T(1,128)S(1)} %get-tuple-element.141), channel_id=1, source_target_pairs={{0,1},{1,2},{2,3},{3,4},{4,5},{5,6},{6,7},{7,8},{8,9},{9,10},{10,1... | collective-permute-start | bytes 584 | tf_op jit(solution)/shard_map/ppermute | solution.py:23
  107.0 7.2 %collective-permute-start.11 = (f32[3,10,1,128]{3,2,1,0:T(1,128)S(1)}, f32[3,10,1,128]{3,2,1,0:T(1,128)S(1)}, u32[]{:S(2)}, u32[]{:S(2)}) collective-permute-start(f32[3,10,1,128]{3,2,1,0:T(1,128)S(1)} %get-tuple-element.52), channel_id=1, source_target_pairs={{1,0},{2,1},{3,2},{4,3},{5,4},{6,5},{7,6},{8,7},{9,8},{10,9},{11,1... | collective-permute-start | bytes 46088 | tf_op jit(solution)/shard_map/ppermute | solution.py:26
  112.2 8.9 %collective-permute-start.10 = (f32[3,10,1,128]{3,2,1,0:T(1,128)S(1)}, f32[3,10,1,128]{3,2,1,0:T(1,128)S(1)}, u32[]{:S(2)}, u32[]{:S(2)}) collective-permute-start(f32[3,10,1,128]{3,2,1,0:T(1,128)S(1)} %get-tuple-element.51), channel_id=1, source_target_pairs={{0,1},{1,2},{2,3},{3,4},{4,5},{5,6},{6,7},{7,8},{8,9},{9,10},{10,1... | collective-permute-start | bytes 46088 | tf_op jit(solution)/shard_map/ppermute | solution.py:23
  143.5 5.0 %collective-permute-start.16 = (f32[3,1,8,64]{3,2,1,0:T(8,128)S(1)}, f32[3,1,8,64]{3,2,1,0:T(8,128)S(1)}, u32[]{:S(2)}, u32[]{:S(2)}) collective-permute-start(f32[3,1,8,64]{3,2,1,0:T(8,128)S(1)} %get-tuple-element.92), channel_id=1, source_target_pairs={{0,128},{128,256},{256,384},{384,512},{512,640},{640,768},{768,896... | collective-permute-start | bytes 18440 | tf_op jit(solution)/shard_map/ppermute | solution.py:23
  148.6 5.9 %collective-permute-start.19 = (f32[3,6,1,64]{3,2,1,0:T(1,128)S(1)}, f32[3,6,1,64]{3,2,1,0:T(1,128)S(1)}, u32[]{:S(2)}, u32[]{:S(2)}) collective-permute-start(f32[3,6,1,64]{3,2,1,0:T(1,128)S(1)} %get-tuple-element.80), channel_id=1, source_target_pairs={{1,0},{2,1},{3,2},{4,3},{5,4},{6,5},{7,6},{8,7},{9,8},{10,9},{11,1... | collective-permute-start | bytes 13832 | tf_op jit(solution)/shard_map/ppermute | solution.py:26
  150.5 8.9 %collective-permute-start.18 = (f32[3,6,1,64]{3,2,1,0:T(1,128)S(1)}, f32[3,6,1,64]{3,2,1,0:T(1,128)S(1)}, u32[]{:S(2)}, u32[]{:S(2)}) collective-permute-start(f32[3,6,1,64]{3,2,1,0:T(1,128)S(1)} %get-tuple-element.79), channel_id=1, source_target_pairs={{0,1},{1,2},{2,3},{3,4},{4,5},{5,6},{6,7},{7,8},{8,9},{9,10},{10,1... | collective-permute-start | bytes 13832 | tf_op jit(solution)/shard_map/ppermute | solution.py:23
  159.9 4.4 %collective-permute-start.21 = (f32[3,1,8,64]{3,2,1,0:T(8,128)S(1)}, f32[3,1,8,64]{3,2,1,0:T(8,128)S(1)}, u32[]{:S(2)}, u32[]{:S(2)}) collective-permute-start(f32[3,1,8,64]{3,2,1,0:T(8,128)S(1)} %get-tuple-element.91), channel_id=1, source_target_pairs={{128,0},{256,128},{384,256},{512,384},{640,512},{768,640},{896,768... | collective-permute-start | bytes 18440 | tf_op jit(solution)/shard_map/ppermute | solution.py:26
  161.8 5.0 %collective-permute-start.20 = (f32[3,1,8,64]{3,2,1,0:T(8,128)S(1)}, f32[3,1,8,64]{3,2,1,0:T(8,128)S(1)}, u32[]{:S(2)}, u32[]{:S(2)}) collective-permute-start(f32[3,1,8,64]{3,2,1,0:T(8,128)S(1)} %get-tuple-element.90), channel_id=1, source_target_pairs={{0,128},{128,256},{256,384},{384,512},{512,640},{640,768},{768,896... | collective-permute-start | bytes 18440 | tf_op jit(solution)/shard_map/ppermute | solution.py:23
  166.8 6.1 %collective-permute-start.23 = (f32[3,6,1,64]{3,2,1,0:T(1,128)S(1)}, f32[3,6,1,64]{3,2,1,0:T(1,128)S(1)}, u32[]{:S(2)}, u32[]{:S(2)}) collective-permute-start(f32[3,6,1,64]{3,2,1,0:T(1,128)S(1)} %get-tuple-element.78), channel_id=1, source_target_pairs={{1,0},{2,1},{3,2},{4,3},{5,4},{6,5},{7,6},{8,7},{9,8},{10,9},{11,1... | collective-permute-start | bytes 13832 | tf_op jit(solution)/shard_map/ppermute | solution.py:26
  168.7 8.9 %collective-permute-start.22 = (f32[3,6,1,64]{3,2,1,0:T(1,128)S(1)}, f32[3,6,1,64]{3,2,1,0:T(1,128)S(1)}, u32[]{:S(2)}, u32[]{:S(2)}) collective-permute-start(f32[3,6,1,64]{3,2,1,0:T(1,128)S(1)} %get-tuple-element.77), channel_id=1, source_target_pairs={{0,1},{1,2},{2,3},{3,4},{4,5},{5,6},{6,7},{7,8},{8,9},{9,10},{10,1... | collective-permute-start | bytes 13832 | tf_op jit(solution)/shard_map/ppermute | solution.py:23
  181.8 4.9 %collective-permute-start.28 = (f32[3,1,4,32]{3,2,1,0:T(4,128)S(1)}, f32[3,1,4,32]{3,2,1,0:T(4,128)S(1)}, u32[]{:S(2)}, u32[]{:S(2)}) collective-permute-start(f32[3,1,4,32]{3,2,1,0:T(4,128)S(1)} %get-tuple-element.127), channel_id=1, source_target_pairs={{0,128},{128,256},{256,384},{384,512},{512,640},{640,768},{768,896... | collective-permute-start | bytes 4616 | tf_op jit(solution)/shard_map/ppermute | solution.py:23
  186.8 5.9 %collective-permute-start.31 = (f32[3,4,1,32]{3,2,1,0:T(1,128)S(1)}, f32[3,4,1,32]{3,2,1,0:T(1,128)S(1)}, u32[]{:S(2)}, u32[]{:S(2)}) collective-permute-start(f32[3,4,1,32]{3,2,1,0:T(1,128)S(1)} %get-tuple-element.109), channel_id=1, source_target_pairs={{1,0},{2,1},{3,2},{4,3},{5,4},{6,5},{7,6},{8,7},{9,8},{10,9},{11,1... | collective-permute-start | bytes 4616 | tf_op jit(solution)/shard_map/ppermute | solution.py:26
  188.7 8.8 %collective-permute-start.30 = (f32[3,4,1,32]{3,2,1,0:T(1,128)S(1)}, f32[3,4,1,32]{3,2,1,0:T(1,128)S(1)}, u32[]{:S(2)}, u32[]{:S(2)}) collective-permute-start(f32[3,4,1,32]{3,2,1,0:T(1,128)S(1)} %get-tuple-element.108), channel_id=1, source_target_pairs={{0,1},{1,2},{2,3},{3,4},{4,5},{5,6},{6,7},{7,8},{8,9},{9,10},{10,1... | collective-permute-start | bytes 4616 | tf_op jit(solution)/shard_map/ppermute | solution.py:23
  199.8 4.9 %collective-permute-start.32 = (f32[3,1,4,32]{3,2,1,0:T(4,128)S(1)}, f32[3,1,4,32]{3,2,1,0:T(4,128)S(1)}, u32[]{:S(2)}, u32[]{:S(2)}) collective-permute-start(f32[3,1,4,32]{3,2,1,0:T(4,128)S(1)} %get-tuple-element.125), channel_id=1, source_target_pairs={{0,128},{128,256},{256,384},{384,512},{512,640},{640,768},{768,896... | collective-permute-start | bytes 4616 | tf_op jit(solution)/shard_map/ppermute | solution.py:23
  204.8 5.9 %collective-permute-start.35 = (f32[3,4,1,32]{3,2,1,0:T(1,128)S(1)}, f32[3,4,1,32]{3,2,1,0:T(1,128)S(1)}, u32[]{:S(2)}, u32[]{:S(2)}) collective-permute-start(f32[3,4,1,32]{3,2,1,0:T(1,128)S(1)} %get-tuple-element.107), channel_id=1, source_target_pairs={{1,0},{2,1},{3,2},{4,3},{5,4},{6,5},{7,6},{8,7},{9,8},{10,9},{11,1... | collective-permute-start | bytes 4616 | tf_op jit(solution)/shard_map/ppermute | solution.py:26
  206.7 8.8 %collective-permute-start.34 = (f32[3,4,1,32]{3,2,1,0:T(1,128)S(1)}, f32[3,4,1,32]{3,2,1,0:T(1,128)S(1)}, u32[]{:S(2)}, u32[]{:S(2)}) collective-permute-start(f32[3,4,1,32]{3,2,1,0:T(1,128)S(1)} %get-tuple-element.106), channel_id=1, source_target_pairs={{0,1},{1,2},{2,3},{3,4},{4,5},{5,6},{6,7},{7,8},{8,9},{9,10},{10,1... | collective-permute-start | bytes 4616 | tf_op jit(solution)/shard_map/ppermute | solution.py:23
  218.0 4.9 %collective-permute-start.40 = (f32[3,1,2,16]{3,2,0,1:T(2,128)S(1)}, f32[3,1,2,16]{3,2,0,1:T(2,128)S(1)}, u32[]{:S(2)}, u32[]{:S(2)}) collective-permute-start(f32[3,1,2,16]{3,2,0,1:T(2,128)S(1)} %bitcast_divide_fusion), channel_id=1, source_target_pairs={{0,128},{128,256},{256,384},{384,512},{512,640},{640,768},{768,896... | collective-permute-start | bytes 1160 | tf_op jit(solution)/shard_map/ppermute | solution.py:23
  223.0 5.9 %collective-permute-start.43 = (f32[3,3,1,16]{3,2,0,1:T(1,128)S(1)}, f32[3,3,1,16]{3,2,0,1:T(1,128)S(1)}, u32[]{:S(2)}, u32[]{:S(2)}) collective-permute-start(f32[3,3,1,16]{3,2,0,1:T(1,128)S(1)} %get-tuple-element.134), channel_id=1, source_target_pairs={{1,0},{2,1},{3,2},{4,3},{5,4},{6,5},{7,6},{8,7},{9,8},{10,9},{11,1... | collective-permute-start | bytes 1736 | tf_op jit(solution)/shard_map/ppermute | solution.py:26
  224.9 8.8 %collective-permute-start.42 = (f32[3,3,1,16]{3,2,0,1:T(1,128)S(1)}, f32[3,3,1,16]{3,2,0,1:T(1,128)S(1)}, u32[]{:S(2)}, u32[]{:S(2)}) collective-permute-start(f32[3,3,1,16]{3,2,0,1:T(1,128)S(1)} %get-tuple-element.133), channel_id=1, source_target_pairs={{0,1},{1,2},{2,3},{3,4},{4,5},{5,6},{6,7},{7,8},{8,9},{9,10},{10,1... | collective-permute-start | bytes 1736 | tf_op jit(solution)/shard_map/ppermute | solution.py:23
  236.0 4.9 %collective-permute-start.44 = (f32[3,1,2,16]{3,2,0,1:T(2,128)S(1)}, f32[3,1,2,16]{3,2,0,1:T(2,128)S(1)}, u32[]{:S(2)}, u32[]{:S(2)}) collective-permute-start(f32[3,1,2,16]{3,2,0,1:T(2,128)S(1)} %get-tuple-element.20), channel_id=1, source_target_pairs={{0,128},{128,256},{256,384},{384,512},{512,640},{640,768},{768,896... | collective-permute-start | bytes 1160 | tf_op jit(solution)/shard_map/ppermute | solution.py:23
  240.9 5.9 %collective-permute-start.47 = (f32[3,3,1,16]{3,2,0,1:T(1,128)S(1)}, f32[3,3,1,16]{3,2,0,1:T(1,128)S(1)}, u32[]{:S(2)}, u32[]{:S(2)}) collective-permute-start(f32[3,3,1,16]{3,2,0,1:T(1,128)S(1)} %get-tuple-element.132), channel_id=1, source_target_pairs={{1,0},{2,1},{3,2},{4,3},{5,4},{6,5},{7,6},{8,7},{9,8},{10,9},{11,1... | collective-permute-start | bytes 1736 | tf_op jit(solution)/shard_map/ppermute | solution.py:26
  242.8 8.8 %collective-permute-start.46 = (f32[3,3,1,16]{3,2,0,1:T(1,128)S(1)}, f32[3,3,1,16]{3,2,0,1:T(1,128)S(1)}, u32[]{:S(2)}, u32[]{:S(2)}) collective-permute-start(f32[3,3,1,16]{3,2,0,1:T(1,128)S(1)} %get-tuple-element.131), channel_id=1, source_target_pairs={{0,1},{1,2},{2,3},{3,4},{4,5},{5,6},{6,7},{7,8},{8,9},{9,10},{10,1... | collective-permute-start | bytes 1736 | tf_op jit(solution)/shard_map/ppermute | solution.py:23
  253.9 4.9 %collective-permute-start.48 = (f32[3,1,2,16]{3,2,0,1:T(2,128)S(1)}, f32[3,1,2,16]{3,2,0,1:T(2,128)S(1)}, u32[]{:S(2)}, u32[]{:S(2)}) collective-permute-start(f32[3,1,2,16]{3,2,0,1:T(2,128)S(1)} %get-tuple-element.18), channel_id=1, source_target_pairs={{0,128},{128,256},{256,384},{384,512},{512,640},{640,768},{768,896... | collective-permute-start | bytes 1160 | tf_op jit(solution)/shard_map/ppermute | solution.py:23
  258.8 5.9 %collective-permute-start.51 = (f32[3,3,1,16]{3,2,0,1:T(1,128)S(1)}, f32[3,3,1,16]{3,2,0,1:T(1,128)S(1)}, u32[]{:S(2)}, u32[]{:S(2)}) collective-permute-start(f32[3,3,1,16]{3,2,0,1:T(1,128)S(1)} %get-tuple-element.130), channel_id=1, source_target_pairs={{1,0},{2,1},{3,2},{4,3},{5,4},{6,5},{7,6},{8,7},{9,8},{10,9},{11,1... | collective-permute-start | bytes 1736 | tf_op jit(solution)/shard_map/ppermute | solution.py:26
  260.7 8.8 %collective-permute-start.50 = (f32[3,3,1,16]{3,2,0,1:T(1,128)S(1)}, f32[3,3,1,16]{3,2,0,1:T(1,128)S(1)}, u32[]{:S(2)}, u32[]{:S(2)}) collective-permute-start(f32[3,3,1,16]{3,2,0,1:T(1,128)S(1)} %get-tuple-element.129), channel_id=1, source_target_pairs={{0,1},{1,2},{2,3},{3,4},{4,5},{5,6},{6,7},{7,8},{8,9},{9,10},{10,1... | collective-permute-start | bytes 1736 | tf_op jit(solution)/shard_map/ppermute | solution.py:23
  272.0 4.9 %collective-permute-start.52 = (f32[3,1,4,32]{3,2,1,0:T(4,128)S(1)}, f32[3,1,4,32]{3,2,1,0:T(4,128)S(1)}, u32[]{:S(2)}, u32[]{:S(2)}) collective-permute-start(f32[3,1,4,32]{3,2,1,0:T(4,128)S(1)} %get-tuple-element.123), channel_id=1, source_target_pairs={{0,128},{128,256},{256,384},{384,512},{512,640},{640,768},{768,896... | collective-permute-start | bytes 4616 | tf_op jit(solution)/shard_map/ppermute | solution.py:23
  277.0 5.9 %collective-permute-start.55 = (f32[3,4,1,32]{3,2,1,0:T(1,128)S(1)}, f32[3,4,1,32]{3,2,1,0:T(1,128)S(1)}, u32[]{:S(2)}, u32[]{:S(2)}) collective-permute-start(f32[3,4,1,32]{3,2,1,0:T(1,128)S(1)} %get-tuple-element.105), channel_id=1, source_target_pairs={{1,0},{2,1},{3,2},{4,3},{5,4},{6,5},{7,6},{8,7},{9,8},{10,9},{11,1... | collective-permute-start | bytes 4616 | tf_op jit(solution)/shard_map/ppermute | solution.py:26
  278.9 8.8 %collective-permute-start.54 = (f32[3,4,1,32]{3,2,1,0:T(1,128)S(1)}, f32[3,4,1,32]{3,2,1,0:T(1,128)S(1)}, u32[]{:S(2)}, u32[]{:S(2)}) collective-permute-start(f32[3,4,1,32]{3,2,1,0:T(1,128)S(1)} %get-tuple-element.104), channel_id=1, source_target_pairs={{0,1},{1,2},{2,3},{3,4},{4,5},{5,6},{6,7},{7,8},{8,9},{9,10},{10,1... | collective-permute-start | bytes 4616 | tf_op jit(solution)/shard_map/ppermute | solution.py:23
  290.0 4.9 %collective-permute-start.56 = (f32[3,1,4,32]{3,2,1,0:T(4,128)S(1)}, f32[3,1,4,32]{3,2,1,0:T(4,128)S(1)}, u32[]{:S(2)}, u32[]{:S(2)}) collective-permute-start(f32[3,1,4,32]{3,2,1,0:T(4,128)S(1)} %get-tuple-element.121), channel_id=1, source_target_pairs={{0,128},{128,256},{256,384},{384,512},{512,640},{640,768},{768,896... | collective-permute-start | bytes 4616 | tf_op jit(solution)/shard_map/ppermute | solution.py:23
  295.0 5.9 %collective-permute-start.59 = (f32[3,4,1,32]{3,2,1,0:T(1,128)S(1)}, f32[3,4,1,32]{3,2,1,0:T(1,128)S(1)}, u32[]{:S(2)}, u32[]{:S(2)}) collective-permute-start(f32[3,4,1,32]{3,2,1,0:T(1,128)S(1)} %get-tuple-element.103), channel_id=1, source_target_pairs={{1,0},{2,1},{3,2},{4,3},{5,4},{6,5},{7,6},{8,7},{9,8},{10,9},{11,1... | collective-permute-start | bytes 4616 | tf_op jit(solution)/shard_map/ppermute | solution.py:26
  296.9 8.8 %collective-permute-start.58 = (f32[3,4,1,32]{3,2,1,0:T(1,128)S(1)}, f32[3,4,1,32]{3,2,1,0:T(1,128)S(1)}, u32[]{:S(2)}, u32[]{:S(2)}) collective-permute-start(f32[3,4,1,32]{3,2,1,0:T(1,128)S(1)} %get-tuple-element.102), channel_id=1, source_target_pairs={{0,1},{1,2},{2,3},{3,4},{4,5},{5,6},{6,7},{7,8},{8,9},{9,10},{10,1... | collective-permute-start | bytes 4616 | tf_op jit(solution)/shard_map/ppermute | solution.py:23
  308.5 5.0 %collective-permute-start.60 = (f32[3,1,8,64]{3,2,1,0:T(8,128)S(1)}, f32[3,1,8,64]{3,2,1,0:T(8,128)S(1)}, u32[]{:S(2)}, u32[]{:S(2)}) collective-permute-start(f32[3,1,8,64]{3,2,1,0:T(8,128)S(1)} %get-tuple-element.88), channel_id=1, source_target_pairs={{0,128},{128,256},{256,384},{384,512},{512,640},{640,768},{768,896... | collective-permute-start | bytes 18440 | tf_op jit(solution)/shard_map/ppermute | solution.py:23
  313.5 5.9 %collective-permute-start.63 = (f32[3,6,1,64]{3,2,1,0:T(1,128)S(1)}, f32[3,6,1,64]{3,2,1,0:T(1,128)S(1)}, u32[]{:S(2)}, u32[]{:S(2)}) collective-permute-start(f32[3,6,1,64]{3,2,1,0:T(1,128)S(1)} %get-tuple-element.76), channel_id=1, source_target_pairs={{1,0},{2,1},{3,2},{4,3},{5,4},{6,5},{7,6},{8,7},{9,8},{10,9},{11,1... | collective-permute-start | bytes 13832 | tf_op jit(solution)/shard_map/ppermute | solution.py:26
  315.4 8.9 %collective-permute-start.62 = (f32[3,6,1,64]{3,2,1,0:T(1,128)S(1)}, f32[3,6,1,64]{3,2,1,0:T(1,128)S(1)}, u32[]{:S(2)}, u32[]{:S(2)}) collective-permute-start(f32[3,6,1,64]{3,2,1,0:T(1,128)S(1)} %get-tuple-element.75), channel_id=1, source_target_pairs={{0,1},{1,2},{2,3},{3,4},{4,5},{5,6},{6,7},{7,8},{8,9},{9,10},{10,1... | collective-permute-start | bytes 13832 | tf_op jit(solution)/shard_map/ppermute | solution.py:23
  326.7 5.0 %collective-permute-start.64 = (f32[3,1,8,64]{3,2,1,0:T(8,128)S(1)}, f32[3,1,8,64]{3,2,1,0:T(8,128)S(1)}, u32[]{:S(2)}, u32[]{:S(2)}) collective-permute-start(f32[3,1,8,64]{3,2,1,0:T(8,128)S(1)} %get-tuple-element.86), channel_id=1, source_target_pairs={{0,128},{128,256},{256,384},{384,512},{512,640},{640,768},{768,896... | collective-permute-start | bytes 18440 | tf_op jit(solution)/shard_map/ppermute | solution.py:23
  331.7 5.9 %collective-permute-start.67 = (f32[3,6,1,64]{3,2,1,0:T(1,128)S(1)}, f32[3,6,1,64]{3,2,1,0:T(1,128)S(1)}, u32[]{:S(2)}, u32[]{:S(2)}) collective-permute-start(f32[3,6,1,64]{3,2,1,0:T(1,128)S(1)} %get-tuple-element.74), channel_id=1, source_target_pairs={{1,0},{2,1},{3,2},{4,3},{5,4},{6,5},{7,6},{8,7},{9,8},{10,9},{11,1... | collective-permute-start | bytes 13832 | tf_op jit(solution)/shard_map/ppermute | solution.py:26
  333.7 8.9 %collective-permute-start.66 = (f32[3,6,1,64]{3,2,1,0:T(1,128)S(1)}, f32[3,6,1,64]{3,2,1,0:T(1,128)S(1)}, u32[]{:S(2)}, u32[]{:S(2)}) collective-permute-start(f32[3,6,1,64]{3,2,1,0:T(1,128)S(1)} %get-tuple-element.73), channel_id=1, source_target_pairs={{0,1},{1,2},{2,3},{3,4},{4,5},{5,6},{6,7},{7,8},{8,9},{9,10},{10,1... | collective-permute-start | bytes 13832 | tf_op jit(solution)/shard_map/ppermute | solution.py:23
  346.0 5.1 %collective-permute-start.68 = (f32[3,1,16,128]{3,2,1,0:T(8,128)S(1)}, f32[3,1,16,128]{3,2,1,0:T(8,128)S(1)}, u32[]{:S(2)}, u32[]{:S(2)}) collective-permute-start(f32[3,1,16,128]{3,2,1,0:T(8,128)S(1)} %get-tuple-element.57), channel_id=1, source_target_pairs={{0,128},{128,256},{256,384},{384,512},{512,640},{640,768},{768,896... | collective-permute-start | bytes 73736 | tf_op jit(solution)/shard_map/ppermute | solution.py:23
  351.2 5.9 %collective-permute-start.71 = (f32[3,10,1,128]{3,2,1,0:T(1,128)S(1)}, f32[3,10,1,128]{3,2,1,0:T(1,128)S(1)}, u32[]{:S(2)}, u32[]{:S(2)}) collective-permute-start(f32[3,10,1,128]{3,2,1,0:T(1,128)S(1)} %get-tuple-element.50), channel_id=1, source_target_pairs={{1,0},{2,1},{3,2},{4,3},{5,4},{6,5},{7,6},{8,7},{9,8},{10,9},{11,1... | collective-permute-start | bytes 46088 | tf_op jit(solution)/shard_map/ppermute | solution.py:26
  353.1 8.9 %collective-permute-start.70 = (f32[3,10,1,128]{3,2,1,0:T(1,128)S(1)}, f32[3,10,1,128]{3,2,1,0:T(1,128)S(1)}, u32[]{:S(2)}, u32[]{:S(2)}) collective-permute-start(f32[3,10,1,128]{3,2,1,0:T(1,128)S(1)} %get-tuple-element.49), channel_id=1, source_target_pairs={{0,1},{1,2},{2,3},{3,4},{4,5},{5,6},{6,7},{7,8},{8,9},{9,10},{10,1... | collective-permute-start | bytes 46088 | tf_op jit(solution)/shard_map/ppermute | solution.py:23
  364.9 5.1 %collective-permute-start.72 = (f32[3,1,16,128]{3,2,1,0:T(8,128)S(1)}, f32[3,1,16,128]{3,2,1,0:T(8,128)S(1)}, u32[]{:S(2)}, u32[]{:S(2)}) collective-permute-start(f32[3,1,16,128]{3,2,1,0:T(8,128)S(1)} %get-tuple-element.55), channel_id=1, source_target_pairs={{0,128},{128,256},{256,384},{384,512},{512,640},{640,768},{768,896... | collective-permute-start | bytes 73736 | tf_op jit(solution)/shard_map/ppermute | solution.py:23
  370.0 5.9 %collective-permute-start.75 = (f32[3,10,1,128]{3,2,1,0:T(1,128)S(1)}, f32[3,10,1,128]{3,2,1,0:T(1,128)S(1)}, u32[]{:S(2)}, u32[]{:S(2)}) collective-permute-start(f32[3,10,1,128]{3,2,1,0:T(1,128)S(1)} %get-tuple-element.48), channel_id=1, source_target_pairs={{1,0},{2,1},{3,2},{4,3},{5,4},{6,5},{7,6},{8,7},{9,8},{10,9},{11,1... | collective-permute-start | bytes 46088 | tf_op jit(solution)/shard_map/ppermute | solution.py:26
  372.0 8.9 %collective-permute-start.74 = (f32[3,10,1,128]{3,2,1,0:T(1,128)S(1)}, f32[3,10,1,128]{3,2,1,0:T(1,128)S(1)}, u32[]{:S(2)}, u32[]{:S(2)}) collective-permute-start(f32[3,10,1,128]{3,2,1,0:T(1,128)S(1)} %get-tuple-element.47), channel_id=1, source_target_pairs={{0,1},{1,2},{2,3},{3,4},{4,5},{5,6},{6,7},{7,8},{8,9},{9,10},{10,1... | collective-permute-start | bytes 46088 | tf_op jit(solution)/shard_map/ppermute | solution.py:23
  (14 other events, 122.3 us)
where the time goes:
time: 385 us; the launch traced here: 382 us
  starting transfers between devices  203 us (53%)
  waiting for transfers between devices  127 us (33%)
  local copies, waits for them, and re-layouts  29.7 us (8%)
  other arithmetic  21 us (5%)
    ppermute x38, waiting for transfers between devices, extended_2(): lax.ppermute(lax.slice_in_dim(block, block.shape[dim] - width, None, axis...  127 us
    ppermute x38, starting transfers between devices, extended_2(): lax.ppermute(lax.slice_in_dim(block, block.shape[dim] - width, None, axis...  113 us
    ppermute x38, starting transfers between devices, extended_2(): lax.ppermute(lax.slice_in_dim(block, 0, width, axis=dim), axis, backward)  90.4 us
    reshape x2, local copies, waits for them, and re-layouts, restrict_field(): values.reshape(values.shape[0], values.shape[1] // 2, 2, values.shape[2]...  15.6 us
    reduce_sum x10, other arithmetic, restrict_field(): return jnp.mean(shaped, axis=(2, 4, 6))  11.4 us
    another operation x2, local copies, waits for them, and re-layouts, restrict_field(): values.reshape(values.shape[0], values.shape[1] // 2, 2, values.shape[2]...  11.1 us
  transfers between devices with their start and end apart: 76, of which 33 were waited for; matrix products, arithmetic and copies ran while one was open for 6% of the time, Pallas kernels for 0%

commit v1 on v0

v1 whole, which is shorter than its diff:
```python
import functools

import jax
import jax.numpy as jnp
from jax import lax
from jax.experimental import pallas as pl
from jax.experimental.pallas import tpu as pltpu
from jax.sharding import PartitionSpec as P

DAMPING = 0.6
COUPLING = 0.2
MASS_TERM = 0.1
PENALTY = 20.0
COARSE_SCALE = 0.25

NL, NB = 8, 128
X0, Y0 = 8, 16
X1, Y1 = 4, 8
H = 3
R0, R1 = Y0 + 8, Y1 + 8
DEEP = 3
GB = 2 * DEEP + 1
MESH = pl.DeviceIdType.MESH
F32 = jnp.float32


def hops(dl, db):
    worst = 0
    for l in range(8):
        dx = abs((l + dl) % 8 // 2 - l // 2)
        for q in range(8):
            dy = abs((q + db) % 8 - q)
            worst = max(worst, min(dx, 4 - dx) + min(dy, 8 - dy) + abs((q + db) // 8))
    return worst


def far_first(pairs):
    return sorted(pairs, key=lambda p: -hops(*p))


NEAR = far_first([(a, b) for a in (-1, 0, 1) for b in (-1, 0, 1) if (a, b) != (0, 0)])
FAR = far_first([(a, b) for a in range(-3, 5) for b in range(-DEEP, DEEP + 1) if (a, b) != (0, 0)])
COLUMN = far_first([(0, b) for b in range(-DEEP - 1, DEEP + 2) if b])
ROW = far_first([(a, 0) for a in range(-3, 5) if a])
GREETED = NEAR + [p for p in FAR + COLUMN if p not in NEAR]
GREETED = [p for i, p in enumerate(GREETED) if p not in GREETED[:i]]


def iota(shape, dim):
    return lax.broadcasted_iota(jnp.int32, shape, dim)


def roll(x, shift, axis):
    size = x.shape[axis]
    return pltpu.roll(x, shift % size, axis % x.ndim)


def smooth_zy(v, step):
    rows = v.shape[-2]
    lane = iota((rows, 128), 1)
    low = jnp.where(lane >= step, 0.5, 0.0).astype(F32)
    high = jnp.where(lane < 128 - step, 0.5, 0.0).astype(F32)
    t = v + low * roll(v, step, -1) + high * roll(v, -step, -1)
    return t + 0.5 * (roll(t, 1, -2) + roll(t, -1, -2))


def smooth(v, step, rows=None):
    t = smooth_zy(v, step)
    if rows is not None:
        t = t[:, :rows]
    return t[1:-1] + 0.5 * (t[:-2] + t[2:])


def sweep(v, c, sides, coeffs, firsts, step, rows=None):
    keep, couple, gain = coeffs
    cut = slice(0, rows)
    mids = [f[1:-1, cut] for f in v]
    drag = COUPLING * (mids[0] + mids[1] + mids[2])
    return [
        keep * mids[k]
        + firsts[k]
        + couple * (smooth(v[k], step, rows) - drag)
        + gain * smooth(c * v[k], step, rows)
        for k in range(3)
    ]


def residual(v, c, c_mid, e_mid, source, step, rows):
    mids = [f[1:-1, :rows] for f in v]
    drag = COUPLING * (mids[0] + mids[1] + mids[2])
    return [
        source[k]
        - e_mid * mids[k]
        + c_mid * (smooth(v[k], step, rows) - drag)
        + smooth(c * v[k], step, rows)
        for k in range(3)
    ]


def swap_pairs(x, step, axis):
    index = iota(x.shape[-2:], 1 if axis in (-1, x.ndim - 1) else 0)
    return jnp.where((index // step) % 2 == 0, roll(x, -step, axis), roll(x, step, axis))


def shift_len(w, by):
    zero = jnp.zeros_like(w[:, :1])
    if by > 0:
        return jnp.concatenate([zero, w[:, :-1]], axis=1)
    return jnp.concatenate([w[:, 1:], zero], axis=1)


def neighbours_y(t, span, padded):
    lane = iota((8, 128), 1)
    up, down = roll(t, -span, -1), (roll(t, span, -1) if span != 64 else None)
    if down is None:
        down = up
    if padded:
        zero = jnp.zeros_like(t[:1])
        up_here, up_next = up, jnp.concatenate([up[1:], zero], axis=0)
        down_here, down_back = down, jnp.concatenate([zero, down[:-1]], axis=0)
    else:
        up_here, up_next = up[1:-1], up[2:]
        down_here, down_back = down[1:-1], down[:-2]
    return jnp.where(lane < 128 - span, up_here, up_next) + jnp.where(lane >= span, down_here, down_back)


def smooth_deep(v, tier, padded):
    step = 1 if tier == 2 else 2
    lane = iota((8, 128), 1)
    low = jnp.where(lane % 32 >= step, 0.5, 0.0).astype(F32)
    high = jnp.where(lane % 32 < 32 - step, 0.5, 0.0).astype(F32)
    t = v + low * roll(v, step, -1) + high * roll(v, -step, -1)
    mid = t if padded else t[1:-1]
    t = mid + 0.5 * neighbours_y(t, 32 if tier == 2 else 64, padded)
    if tier == 2:
        first = iota((8, 128), 0) % 2 == 0
        w = swap_pairs(t, 1, -2)
        beside = w + jnp.where(first, shift_len(w, 1), shift_len(w, -1))
    else:
        beside = shift_len(t, 1) + shift_len(t, -1)
    return t + 0.5 * beside


def sum_deep(v):
    u = v + roll(v, 2, -2)
    return u + roll(u, 4, -2)


def body(
    forces, modulus, occupancy, bonded, out, raw, mod_v, occ_v, bon_v, cs1, b1, v2a, v2b, first0, first1, co0, co1,
    pair, cs2, b2, sent2, co2, co3, e2, pe2, pe1,
    load_sem, send_a, recv_a, send_b, recv_b, send_k, recv_k, send_v, recv_v, send_w, recv_w,
    send_g, recv_g, send_h, recv_h, send_d, recv_d,
):
    me_l, me_b = lax.axis_index("len"), lax.axis_index("brick")

    def device(dl, db):
        return (lax.rem(me_l + dl + NL, NL), lax.rem(me_b + db + NB, NB))

    loads = [
        pltpu.make_async_copy(modulus, mod_v, load_sem.at[0]),
        pltpu.make_async_copy(occupancy, occ_v, load_sem.at[1]),
        pltpu.make_async_copy(bonded, bon_v, load_sem.at[2]),
        pltpu.make_async_copy(forces, raw.at[pl.ds(0, 3), pl.ds(H, X0), pl.ds(0, Y0), :], load_sem.at[3]),
    ]
    for load in loads:
        load.start()
    barrier = pltpu.get_barrier_semaphore()
    for dl, db in GREETED:
        pl.semaphore_signal(barrier, inc=1, device_id=device(dl, db), device_id_type=MESH)

    def exchange(buf, sends, recvs, width, size_x, size_y, rows, off):
        copies = []
        for i, (dl, db) in enumerate(NEAR):
            xs, xd, nx = {
                0: (off, off, size_x),
                1: (off + size_x - width, off - width, width),
                -1: (off, off + size_x, width),
            }[dl]
            ys, yd, ny = {
                0: (0, 0, size_y),
                1: (size_y - width, rows - width, width),
                -1: (0, size_y, width),
            }[db]
            copy = pltpu.make_async_remote_copy(
                src_ref=buf.at[:, pl.ds(xs, nx), pl.ds(ys, ny), :],
                dst_ref=buf.at[:, pl.ds(xd, nx), pl.ds(yd, ny), :],
                send_sem=sends.at[i],
                recv_sem=recvs.at[i],
                device_id=device(dl, db),
                device_id_type=MESH,
            )
            copy.start()
            copies.append(copy)
        return copies

    def arrive(copies):
        for copy in copies:
            copy.wait_recv()

    def leave(copies):
        for copy in copies:
            copy.wait_send()

    one, zero = jnp.float32(1.0), jnp.float32(0.0)
    low_x = jnp.where(me_l > 0, one, zero)
    high_x = jnp.where(me_l < NL - 1, one, zero)
    low_y = jnp.where(me_b > 0, one, zero)
    high_y = jnp.where(me_b < NB - 1, one, zero)

    def inside(n_local, halo, rows, y_local):
        row = iota((rows, 128), 0)
        in_y = jnp.where(row < y_local, one, jnp.where(row < y_local + 4, high_y, low_y))
        parts = [jnp.broadcast_to((in_y * low_x)[None], (halo, rows, 128))]
        parts.append(jnp.broadcast_to(in_y[None], (n_local, rows, 128)))
        parts.append(jnp.broadcast_to((in_y * high_x)[None], (halo, rows, 128)))
        return jnp.concatenate(parts, axis=0)

    for load in loads[:3]:
        load.wait()
    c_here = mod_v[...] * occ_v[...].astype(F32)
    s_here = MASS_TERM + PENALTY * bon_v[...].astype(F32)
    raw[3, H : H + X0, 0:Y0, :] = s_here
    raw[4, H : H + X0, 0:Y0, :] = c_here
    loads[3].wait()
    pl.semaphore_wait(barrier, len(GREETED))
    copies_a = exchange(raw, send_a, recv_a, H, X0, Y0, R0, H)

    def halve(fields):
        result = []
        for k, f in enumerate(fields):
            f = f.reshape(X1, 2, Y0, 128)
            pair[k] = f[:, 0] + f[:, 1]
            u = pair[k, :, pl.ds(0, Y1, stride=2), :] + pair[k, :, pl.ds(1, Y1, stride=2), :]
            result.append(0.125 * (u + swap_pairs(u, 1, -1)))
        return result

    def flatten(fields):
        stacked = [f.reshape(2, 2, Y1, 128) for f in fields]
        stacked = jnp.concatenate([f[:, 0] + f[:, 1] for f in stacked], axis=0)
        n = stacked.shape[0]
        a, b = iota((128, 128), 0), iota((128, 128), 1)
        squeeze = jnp.where(a // 4 == b % 32, 0.0625, 0.0).astype(F32)
        t = jnp.dot(
            stacked.reshape(n * 8, 128), squeeze, precision=lax.Precision.HIGHEST, preferred_element_type=F32
        ).reshape(n, 8, 128)
        t = jnp.where(iota((8, 128), 1) // 32 == iota((8, 128), 0) // 2, t, 0.0)
        t = t + roll(t, 4, -2)
        t = t + roll(t, 2, -2)
        return t + roll(t, 1, -2)

    c1_here, s1_here = halve([c_here, s_here])
    c1_here = COARSE_SCALE * c1_here
    cs1[0, H : H + X1, 0:Y1, :] = s1_here
    cs1[1, H : H + X1, 0:Y1, :] = c1_here
    copies_k = exchange(cs1, send_k, recv_k, H, X1, Y1, R1, H)
    four = flatten([COARSE_SCALE * c1_here, s1_here])
    row8 = iota((8, 128), 0)
    tile = four[0]
    for k in range(1, 4):
        tile = jnp.where(row8 % 4 == k, four[k], tile)
    cs2[DEEP + 1, pl.ds(me_l, 1)] = tile[None]
    copies_g = []
    for i, (dl, db) in enumerate(COLUMN):
        copy = pltpu.make_async_remote_copy(
            src_ref=cs2.at[DEEP + 1, pl.ds(me_l, 1)],
            dst_ref=cs2.at[DEEP + 1 - db, pl.ds(me_l, 1)],
            send_sem=send_g.at[i],
            recv_sem=recv_g.at[i],
            device_id=device(dl, db),
            device_id_type=MESH,
        )
        copy.start()
        copies_g.append(copy)

    def coefficients(buf, store, n_local, rows, y_local, step):
        mask3 = inside(n_local, 3, rows, y_local)
        n_f = buf.shape[0]
        c = jnp.where(mask3 > 0.5, buf[n_f - 1], 0.0)
        c_mid = c[1:-1]
        plus = smooth(c, step) + buf[n_f - 2, 1:-1]
        e = 8.0 * c_mid + plus
        g = DAMPING * mask3[1:-1] / (6.2 * c_mid + plus)
        store[0] = 1.0 - g * e
        store[1] = g * c_mid
        store[2] = g
        store[3] = c_mid
        store[4] = e
        buf[n_f - 1] = c

    arrive(copies_a)
    leave(copies_a)
    coefficients(raw, co0, X0, R0, Y0, 1)
    gain = co0[2]
    v1 = [gain * raw[k, 1:-1] for k in range(3)]
    for k in range(3):
        first0[k] = v1[k]
    c_12 = co0[3]
    inner = [co0[k, 1:-1] for k in range(3)]
    v2 = sweep(v1, c_12, None, inner, [f[1:-1] for f in v1], 1)
    for k in range(3):
        v2a[k, 2 : 2 + X0, 0:Y0, :] = v2[k][1:-1, :Y0]
    r0 = residual(
        v2, c_12[1:-1], co0[3, 2:-2, :Y0], co0[4, 2:-2, :Y0], [raw[k, H : H + X0, :Y0] for k in range(3)], 1, Y0
    )
    for k, f in enumerate(halve(r0)):
        b1[k, H : H + X1, 0:Y1, :] = f
    copies_b = exchange(b1, send_b, recv_b, 2, X1, Y1, R1, H)
    copies_v = exchange(v2a, send_v, recv_v, 2, X0, Y0, R0, 2)

    arrive(copies_g)
    copies_h = []
    for i, (dl, db) in enumerate(ROW):
        copy = pltpu.make_async_remote_copy(
            src_ref=cs2.at[:, pl.ds(me_l, 1)],
            dst_ref=cs2.at[:, pl.ds(me_l, 1)],
            send_sem=send_h.at[i],
            recv_sem=recv_h.at[i],
            device_id=device(dl, db),
            device_id_type=MESH,
        )
        copy.start()
        copies_h.append(copy)

    arrive(copies_k)
    leave(copies_k)
    coefficients(cs1, co1, X1, R1, Y1, 2)
    arrive(copies_b)
    gain = co1[2]
    v1 = [gain * b1[k, 1:-1] for k in range(3)]
    for k in range(3):
        first1[k] = v1[k]
    c_8 = co1[3]
    inner = [co1[k, 1:-1] for k in range(3)]
    v2 = sweep(v1, c_8, None, inner, [f[1:-1] for f in v1], 2)
    for k in range(3):
        v2b[k, H : H + X1, 0:Y1, :] = v2[k][1:-1, :Y1]
    r1 = residual(
        v2, c_8[1:-1], co1[3, 2:-2, :Y1], co1[4, 2:-2, :Y1], [b1[k, H : H + X1, :Y1] for k in range(3)], 2, Y1
    )
    six = flatten(r1)
    tile = jnp.where(row8 == 0, six[0], 0.0)
    for k in range(1, 6):
        tile = jnp.where(row8 == k, six[k], tile)
    sent2[0] = tile
    b2[pl.ds(DEEP * NL + me_l, 1)] = tile[None]
    for dl, db in FAR:
        pltpu.make_async_remote_copy(
            src_ref=sent2,
            dst_ref=b2.at[pl.ds((DEEP - db) * NL + me_l, 1)],
            send_sem=send_d.at[0],
            recv_sem=recv_d.at[0],
            device_id=device(dl, db),
            device_id_type=MESH,
        ).start()
    copies_w = exchange(v2b, send_w, recv_w, H, X1, Y1, R1, H)

    arrive(copies_h)
    leave(copies_h)
    leave(copies_g)
    leave(copies_b)
    leave(copies_v)
    u = cs2[...]
    w = roll(u, 2, -2)
    is_c = (row8 // 2) % 2 == 0
    valid = []
    for b in range(-DEEP - 1, DEEP + 2):
        ok = jnp.logical_and(me_b + b >= 0, me_b + b < NB)
        valid.append(jnp.broadcast_to(jnp.where(ok, one, zero), (1, 1, 8, 128)))
    valid = jnp.concatenate(valid, axis=0)
    c2 = jnp.where(is_c, u, w) * valid
    s2 = jnp.where(is_c, w, u)[1:-1]
    live = valid[1:-1] * jnp.where(row8 < 6, 1.0, 0.0).astype(F32)

    def deep_coefficients(c, smoothed, s, store):
        plus = smoothed + s
        e = 8.0 * c + plus
        g = DAMPING * live / (6.2 * c + plus)
        store[0] = 1.0 - g * e
        store[1] = g * c
        store[2] = g
        store[3] = c
        store[4] = e

    def restrict_deep(v):
        v = v + swap_pairs(v, 1, -2)
        v = v + swap_pairs(v, 32, -1)
        return 0.125 * (v + swap_pairs(v, 1, -1))

    deep_coefficients(c2[1:-1], smooth_deep(c2, 2, False), s2, co2)
    c3 = COARSE_SCALE * restrict_deep(c2[1:-1])
    deep_coefficients(c3, smooth_deep(c3, 3, True), restrict_deep(s2), co3)

    pltpu.make_async_copy(b2.at[pl.ds(0, len(FAR))], b2.at[pl.ds(0, len(FAR))], recv_d.at[0]).wait()

    def deep_sweep(v, store, tier, first, padded, lo, hi):
        mid = v if padded else v[1:-1]
        c = store[3, lo:hi] if padded else store[3, lo - 1 : hi + 1]
        drag = COUPLING * sum_deep(mid)
        return (
            store[0, lo:hi] * mid
            + first
            + store[1, lo:hi] * (smooth_deep(v, tier, padded) - drag)
            + store[2, lo:hi] * smooth_deep(c * v, tier, padded)
        )

    source = b2[...].reshape(GB, NL, 8, 128)
    v1 = co2[2] * source
    v2 = deep_sweep(v1, co2, 2, v1, True, 0, GB)
    c = co2[3]
    r2 = source - co2[4] * v2 + c * (smooth_deep(v2, 2, True) - COUPLING * sum_deep(v2)) + smooth_deep(c * v2, 2, True)
    f3 = co3[2] * restrict_deep(r2)
    v = deep_sweep(f3, co3, 3, f3[1:-1], False, 1, GB - 1)
    v = deep_sweep(v, co3, 3, f3[1:-1], True, 1, GB - 1)
    v = deep_sweep(v, co3, 3, f3[2:-2], False, 2, GB - 2)
    near = slice(DEEP - 1, DEEP + 2)
    v = v2[near] + v
    v = deep_sweep(v, co2, 2, v1[near], True, DEEP - 1, DEEP + 2)
    v = deep_sweep(v, co2, 2, v1[near], True, DEEP - 1, DEEP + 2)

    e2[:, 0:1] = jnp.zeros((3, 1, 8, 128), F32)
    e2[:, NL + 1 : NL + 2] = jnp.zeros((3, 1, 8, 128), F32)
    e2[:, 1 : NL + 1] = v
    rows72 = e2[:, pl.ds(me_l, 3)].reshape(72, 128)
    a, b = iota((128, 128), 0), iota((128, 128), 1)
    for y in range(4):
        spread = jnp.where(a == 32 * y + b // 4, 1.0, 0.0).astype(F32)
        pe2[y] = jnp.dot(rows72, spread, precision=lax.Precision.HIGHEST, preferred_element_type=F32)

    def coarse_rows(k, x2):
        group, parity = x2 // 2 + 1, x2 % 2

        def spread_row(brick, y):
            start = (brick * 3 + group) * 8 + k * 2 + parity
            return pe2[y, pl.ds(start, 8, stride=0), :]

        here = spread_row(1, 0)
        for y in range(1, 4):
            here = jnp.where(row8 // 2 == y, spread_row(1, y), here)
        halo = spread_row(2, 0)
        halo = jnp.where(row8 // 2 == 1, spread_row(2, 1), halo)
        halo = jnp.where(row8 // 2 == 2, spread_row(0, 2), halo)
        halo = jnp.where(row8 // 2 == 3, spread_row(0, 3), halo)
        return jnp.concatenate([here, halo], axis=0)

    up = []
    for k in range(3):
        cells = {x2: coarse_rows(k, x2) for x2 in range(-2, 4)}
        up.append(jnp.stack([cells[x // 2] for x in range(-H, X1 + H)], axis=0))
    arrive(copies_w)
    held = inside(X1, H, R1, Y1) > 0.5
    v = [jnp.where(held, v2b[k], 0.0) + up[k] for k in range(3)]
    v = sweep(v, cs1[1], None, [co1[k] for k in range(3)], [first1[k] for k in range(3)], 2)
    inner = [co1[k, 1:-1] for k in range(3)]
    v = sweep(v, co1[3], None, inner, [first1[k, 1:-1] for k in range(3)], 2)

    for k in range(3):
        pe1[k, :, pl.ds(0, Y1, stride=2), :] = v[k][:, :Y1]
        pe1[k, :, pl.ds(1, Y1, stride=2), :] = v[k][:, :Y1]
        t = v[k][:, Y1:]
        pe1[k, :, Y0:R0, :] = jnp.where(row8 == 1, roll(t, 1, -2), jnp.where(row8 == 6, roll(t, -1, -2), t))
    arrive(copies_v)
    up = []
    held = co0[2] > 0.0
    for k in range(3):
        e = pe1[k]
        up.append(jnp.where(held, v2a[k], 0.0) + jnp.broadcast_to(e[:, None], (6, 2, R0, 128)).reshape(12, R0, 128))
    c_12 = co0[3]
    v = sweep(up, c_12, None, [co0[k, 1:-1] for k in range(3)], [first0[k, 1:-1] for k in range(3)], 1)
    inner = [co0[k, 2:-2, :Y0] for k in range(3)]
    v = sweep(v, c_12[1:-1], None, inner, [first0[k, 2:-2, :Y0] for k in range(3)], 1, Y0)
    for k in range(3):
        out[k] = v[k]
    leave(copies_w)
    pltpu.make_async_copy(b2.at[pl.ds(0, len(FAR))], b2.at[pl.ds(0, len(FAR))], send_d.at[0]).wait()


def cycle(forces, modulus, occupancy, bonded):
    dma = pltpu.SemaphoreType.DMA
    vmem = pltpu.VMEM
    return pl.pallas_call(
        body,
        out_shape=jax.ShapeDtypeStruct((3, X0, Y0, 128), F32),
        in_specs=[pl.BlockSpec(memory_space=pl.ANY)] * 4,
        out_specs=pl.BlockSpec(memory_space=pltpu.VMEM),
        scratch_shapes=[
            vmem((5, X0 + 2 * H, R0, 128), F32),
            vmem((X0, Y0, 128), F32),
            vmem((X0, Y0, 128), jnp.int32),
            vmem((X0, Y0, 128), jnp.int32),
            vmem((2, X1 + 2 * H, R1, 128), F32),
            vmem((3, X1 + 2 * H, R1, 128), F32),
            vmem((3, X0 + 4, R0, 128), F32),
            vmem((3, X1 + 2 * H, R1, 128), F32),
            vmem((3, X0 + 4, R0, 128), F32),
            vmem((3, X1 + 4, R1, 128), F32),
            vmem((5, X0 + 4, R0, 128), F32),
            vmem((5, X1 + 4, R1, 128), F32),
            vmem((3, X1, Y0, 128), F32),
            vmem((GB + 2, NL, 8, 128), F32),
            vmem((GB * NL, 8, 128), F32),
            vmem((1, 8, 128), F32),
            vmem((5, GB, NL, 8, 128), F32),
            vmem((5, GB, NL, 8, 128), F32),
            vmem((3, NL + 2, 8, 128), F32),
            vmem((4, 72, 128), F32),
            vmem((3, 6, R0, 128), F32),
            dma((4,)),
            dma((8,)), dma((8,)), dma((8,)), dma((8,)), dma((8,)), dma((8,)), dma((8,)), dma((8,)), dma((8,)), dma((8,)),
            dma((len(COLUMN),)), dma((len(COLUMN),)), dma((len(ROW),)), dma((len(ROW),)), dma((1,)), dma((1,)),
        ],
        compiler_params=pltpu.CompilerParams(collective_id=0, has_side_effects=True, vmem_limit_bytes=48 << 20),
    )(forces, modulus, occupancy, bonded)


def solution(mesh):
    in_specs = (
        P(None, "len", "brick", None),
        P("len", "brick", None),
        P("len", "brick", None),
        P("len", "brick", None),
    )
    out_specs = P(None, "len", "brick", None)
    return jax.shard_map(cycle, mesh=mesh, in_specs=in_specs, out_specs=out_specs, check_vma=False)
```

time: 385 us -> 56.6 us (0.15)
  the two profiles are of different devices: /device:TPU:774 before, /device:TPU:1 now
where the time goes in v1:
time: 56.6 us; the launch traced here: 56.3 us
  Pallas kernels  52.2 us (92%)
  local copies, waits for them, and re-layouts  4.12 us (7%)
    pallas_call x1, Pallas kernels, cycle(): pl.pallas_call(body, out_shape=jax.ShapeDtypeStruct((3, X0, Y0, 128), F32...  52.2 us
    unnamed x9, local copies, waits for them, and re-layouts  4.12 us

profile of v1, /device:TPU:1, one launch (start us, length us, event | category | flops | bytes accessed | tf_op | source)
XLA Modules:
  0.0 56.3 jit_solution(17999000118357131735)
XLA Ops:
  0.0 0.0 copy-start
  0.0 0.9 %copy-done = f32[3,8,16,128]{3,2,1,0:T(8,128)S(1)} copy-done((f32[3,8,16,128]{3,2,1,0:T(8,128)S(1)}, f32[3,8,16,128]{3,2,1,0:T(8,128)}, u32[]{:S(2)}) %copy-start) | copy-done | bytes 196632
  0.9 0.0 copy-start.1
  0.9 0.8 %copy-done.1 = f32[8,16,128]{2,1,0:T(8,128)S(1)} copy-done((f32[8,16,128]{2,1,0:T(8,128)S(1)}, f32[8,16,128]{2,1,0:T(8,128)}, u32[]{:S(2)}) %copy-start.1) | copy-done | bytes 65560
  1.8 0.0 copy-start.2
  1.8 0.8 %copy-done.2 = s32[8,16,128]{2,1,0:T(8,128)S(1)} copy-done((s32[8,16,128]{2,1,0:T(8,128)S(1)}, s32[8,16,128]{2,1,0:T(8,128)}, u32[]{:S(2)}) %copy-start.2) | copy-done | bytes 65560
  2.6 0.0 copy-start.3
  2.6 0.8 %copy-done.3 = s32[8,16,128]{2,1,0:T(8,128)S(1)} copy-done((s32[8,16,128]{2,1,0:T(8,128)S(1)}, s32[8,16,128]{2,1,0:T(8,128)}, u32[]{:S(2)}) %copy-start.3) | copy-done | bytes 65560
  3.4 52.2 %shard_map.46 = f32[3,8,16,128]{3,2,1,0:T(8,128)S(1)} custom-call(f32[3,8,16,128]{3,2,1,0:T(8,128)S(1)} %copy-done, f32[8,16,128]{2,1,0:T(8,128)S(1)} %copy-done.1, s32[8,16,128]{2,1,0:T(8,128)S(1)} %copy-done.2, s32[8,16,128]{2,1,0:T(8,128)S(1)} %copy-done.3), custom_call_target="tpu_custom_call" | custom-call | tf_op jit(solution)/shard_map/pallas_call | solution.py:481
  55.6 0.7 %copy.6 = f32[3,8,16,128]{3,2,1,0:T(8,128)} copy(f32[3,8,16,128]{3,2,1,0:T(8,128)S(1)} %shard_map.46) | data formatting | bytes 393216
Async XLA Ops:
  0.0 0.9 %copy-start = (f32[3,8,16,128]{3,2,1,0:T(8,128)S(1)}, f32[3,8,16,128]{3,2,1,0:T(8,128)}, u32[]{:S(2)}) copy-start(f32[3,8,16,128]{3,2,1,0:T(8,128)} %forces.1) | copy-start | bytes 589828
  0.9 0.8 %copy-start.1 = (f32[8,16,128]{2,1,0:T(8,128)S(1)}, f32[8,16,128]{2,1,0:T(8,128)}, u32[]{:S(2)}) copy-start(f32[8,16,128]{2,1,0:T(8,128)} %modulus.1) | copy-start | bytes 196612
  1.8 0.8 %copy-start.2 = (s32[8,16,128]{2,1,0:T(8,128)S(1)}, s32[8,16,128]{2,1,0:T(8,128)}, u32[]{:S(2)}) copy-start(s32[8,16,128]{2,1,0:T(8,128)} %occupancy.1) | copy-start | bytes 196612
  2.6 0.8 %copy-start.3 = (s32[8,16,128]{2,1,0:T(8,128)S(1)}, s32[8,16,128]{2,1,0:T(8,128)}, u32[]{:S(2)}) copy-start(s32[8,16,128]{2,1,0:T(8,128)} %bonded.1) | copy-start | bytes 196612

commit v2 on v1

--- a/solution.py
+++ b/solution.py
@@ -38,12 +38,11 @@
     return sorted(pairs, key=lambda p: -hops(*p))
 
 
-NEAR = far_first([(a, b) for a in (-1, 0, 1) for b in (-1, 0, 1) if (a, b) != (0, 0)])
-FAR = far_first([(a, b) for a in range(-3, 5) for b in range(-DEEP, DEEP + 1) if (a, b) != (0, 0)])
+NEAR = [(a, b) for b in (1, -1, 0) for a in (1, -1, 0) if (a, b) != (0, 0)]
+FAR = [p for d in range(DEEP, -1, -1) for b in {d, -d} for p in far_first([(a, b) for a in range(-3, 5) if (a, b) != (0, 0)])]
 COLUMN = far_first([(0, b) for b in range(-DEEP - 1, DEEP + 2) if b])
 ROW = far_first([(a, 0) for a in range(-3, 5) if a])
-GREETED = NEAR + [p for p in FAR + COLUMN if p not in NEAR]
-GREETED = [p for i, p in enumerate(GREETED) if p not in GREETED[:i]]
+GREETED = NEAR + [(4, 0), (4, 1), (4, -1)] + [p for p in COLUMN if p not in NEAR]
 
 
 def iota(shape, dim):
@@ -165,9 +164,56 @@
     ]
     for load in loads:
         load.start()
+    def exists(db):
+        return jnp.logical_and(me_b + db >= 0, me_b + db < NB)
+
+    def where_exists(db, act):
+        if db == 0:
+            act()
+        else:
+            pl.when(exists(db))(act)
+
+    def by_brick(pairs):
+        groups = {}
+        for i, (dl, db) in enumerate(pairs):
+            groups.setdefault(db, []).append((i, dl))
+        return groups.items()
+
     barrier = pltpu.get_barrier_semaphore()
-    for dl, db in GREETED:
-        pl.semaphore_signal(barrier, inc=1, device_id=device(dl, db), device_id_type=MESH)
+    for db, group in by_brick(GREETED):
+
+        def greet(db=db, group=group):
+            for _, dl in group:
+                pl.semaphore_signal(barrier, inc=1, device_id=device(dl, db), device_id_type=MESH)
+
+        where_exists(db, greet)
+
+    def start(pairs, copies):
+        for db, group in by_brick(pairs):
+
+            def go(group=group):
+                for i, _ in group:
+                    copies[i].start()
+
+            where_exists(db, go)
+
+    def arrive(pairs, copies):
+        for db, group in by_brick(pairs):
+
+            def done(group=group):
+                for i, _ in group:
+                    copies[i].wait_recv()
+
+            where_exists(-db, done)
+
+    def leave(pairs, copies):
+        for db, group in by_brick(pairs):
+
+            def done(group=group):
+                for i, _ in group:
+                    copies[i].wait_send()
+
+            where_exists(db, done)
 
     def exchange(buf, sends, recvs, width, size_x, size_y, rows, off):
         copies = []
@@ -182,25 +228,29 @@
                 1: (size_y - width, rows - width, width),
                 -1: (0, size_y, width),
             }[db]
-            copy = pltpu.make_async_remote_copy(
-                src_ref=buf.at[:, pl.ds(xs, nx), pl.ds(ys, ny), :],
-                dst_ref=buf.at[:, pl.ds(xd, nx), pl.ds(yd, ny), :],
-                send_sem=sends.at[i],
-                recv_sem=recvs.at[i],
-                device_id=device(dl, db),
-                device_id_type=MESH,
+            copies.append(
+                pltpu.make_async_remote_copy(
+                    src_ref=buf.at[:, pl.ds(xs, nx), pl.ds(ys, ny), :],
+                    dst_ref=buf.at[:, pl.ds(xd, nx), pl.ds(yd, ny), :],
+                    send_sem=sends.at[i],
+                    recv_sem=recvs.at[i],
+                    device_id=device(dl, db),
+                    device_id_type=MESH,
+                )
             )
-            copy.start()
-            copies.append(copy)
+        start(NEAR, copies)
         return copies
 
-    def arrive(copies):
-        for copy in copies:
-            copy.wait_recv()
-
-    def leave(copies):
-        for copy in copies:
-            copy.wait_send()
+    def clear(buf, rows, y_local):
+        @pl.when(me_b == 0)
+        def _():
+            shape = buf.shape[:2] + (rows - y_local - 3, 128)
+            buf[:, :, y_local + 3 :, :] = jnp.ones(shape, F32)
+
+        @pl.when(me_b == NB - 1)
+        def _():
+            shape = buf.shape[:2] + (rows - y_local - 3, 128)
+            buf[:, :, y_local : rows - 3, :] = jnp.ones(shape, F32)
 
     one, zero = jnp.float32(1.0), jnp.float32(0.0)
     low_x = jnp.where(me_l > 0, one, zero)
@@ -223,8 +273,23 @@
     raw[3, H : H + X0, 0:Y0, :] = s_here
     raw[4, H : H + X0, 0:Y0, :] = c_here
     loads[3].wait()
-    pl.semaphore_wait(barrier, len(GREETED))
+    greeters = jnp.int32(0)
+    for db, group in by_brick(GREETED):
+        greeters = greeters + (len(group) if db == 0 else len(group) * exists(db).astype(jnp.int32))
+    pl.semaphore_wait(barrier, greeters)
     copies_a = exchange(raw, send_a, recv_a, H, X0, Y0, R0, H)
+    clear(raw, R0, Y0)
+    clear(cs1, R1, Y1)
+    clear(b1, R1, Y1)
+    for db in range(-DEEP - 1, DEEP + 2):
+        if db:
+
+            @pl.when(jnp.logical_not(exists(db)))
+            def _(db=db):
+                cs2[DEEP + 1 + db, pl.ds(me_l, 1)] = jnp.ones((1, 8, 128), F32)
+                if abs(db) <= DEEP:
+                    b2[pl.ds((DEEP + db) * NL, NL)] = jnp.zeros((NL, 8, 128), F32)
+
 
     def halve(fields):
         result = []
@@ -270,8 +335,8 @@
             device_id=device(dl, db),
             device_id_type=MESH,
         )
-        copy.start()
         copies_g.append(copy)
+    start(COLUMN, copies_g)
 
     def coefficients(buf, store, n_local, rows, y_local, step):
         mask3 = inside(n_local, 3, rows, y_local)
@@ -288,8 +353,8 @@
         store[4] = e
         buf[n_f - 1] = c
 
-    arrive(copies_a)
-    leave(copies_a)
+    arrive(NEAR, copies_a)
+    leave(NEAR, copies_a)
     coefficients(raw, co0, X0, R0, Y0, 1)
     gain = co0[2]
     v1 = [gain * raw[k, 1:-1] for k in range(3)]
@@ -308,7 +373,7 @@
     copies_b = exchange(b1, send_b, recv_b, 2, X1, Y1, R1, H)
     copies_v = exchange(v2a, send_v, recv_v, 2, X0, Y0, R0, 2)
 
-    arrive(copies_g)
+    arrive(COLUMN, copies_g)
     copies_h = []
     for i, (dl, db) in enumerate(ROW):
         copy = pltpu.make_async_remote_copy(
@@ -319,13 +384,13 @@
             device_id=device(dl, db),
             device_id_type=MESH,
         )
-        copy.start()
         copies_h.append(copy)
-
-    arrive(copies_k)
-    leave(copies_k)
+    start(ROW, copies_h)
+
+    arrive(NEAR, copies_k)
+    leave(NEAR, copies_k)
     coefficients(cs1, co1, X1, R1, Y1, 2)
-    arrive(copies_b)
+    arrive(NEAR, copies_b)
     gain = co1[2]
     v1 = [gain * b1[k, 1:-1] for k in range(3)]
     for k in range(3):
@@ -344,29 +409,43 @@
         tile = jnp.where(row8 == k, six[k], tile)
     sent2[0] = tile
     b2[pl.ds(DEEP * NL + me_l, 1)] = tile[None]
-    for dl, db in FAR:
-        pltpu.make_async_remote_copy(
-            src_ref=sent2,
-            dst_ref=b2.at[pl.ds((DEEP - db) * NL + me_l, 1)],
-            send_sem=send_d.at[0],
-            recv_sem=recv_d.at[0],
-            device_id=device(dl, db),
-            device_id_type=MESH,
-        ).start()
+    for db, group in by_brick(FAR):
+
+        def spread(db=db, group=group):
+            for _, dl in group:
+                pltpu.make_async_remote_copy(
+                    src_ref=sent2,
+                    dst_ref=b2.at[pl.ds((DEEP - db) * NL + me_l, 1)],
+                    send_sem=send_d.at[DEEP + db],
+                    recv_sem=recv_d.at[DEEP - db],
+                    device_id=device(dl, db),
+                    device_id_type=MESH,
+                ).start()
+
+        where_exists(db, spread)
+
+    def await_far(sems):
+        for db, group in by_brick(FAR):
+
+            def done(db=db, count=len(group)):
+                held = b2.at[pl.ds(0, count)]
+                pltpu.make_async_copy(held, held, sems.at[DEEP + db]).wait()
+
+            where_exists(db, done)
+
     copies_w = exchange(v2b, send_w, recv_w, H, X1, Y1, R1, H)
 
-    arrive(copies_h)
-    leave(copies_h)
-    leave(copies_g)
-    leave(copies_b)
-    leave(copies_v)
+    arrive(ROW, copies_h)
+    leave(ROW, copies_h)
+    leave(COLUMN, copies_g)
+    leave(NEAR, copies_b)
+    leave(NEAR, copies_v)
     u = cs2[...]
     w = roll(u, 2, -2)
     is_c = (row8 // 2) % 2 == 0
     valid = []
     for b in range(-DEEP - 1, DEEP + 2):
-        ok = jnp.logical_and(me_b + b >= 0, me_b + b < NB)
-        valid.append(jnp.broadcast_to(jnp.where(ok, one, zero), (1, 1, 8, 128)))
+        valid.append(jnp.broadcast_to(jnp.where(exists(b), one, zero), (1, 1, 8, 128)))
     valid = jnp.concatenate(valid, axis=0)
     c2 = jnp.where(is_c, u, w) * valid
     s2 = jnp.where(is_c, w, u)[1:-1]
@@ -391,7 +470,7 @@
     c3 = COARSE_SCALE * restrict_deep(c2[1:-1])
     deep_coefficients(c3, smooth_deep(c3, 3, True), restrict_deep(s2), co3)
 
-    pltpu.make_async_copy(b2.at[pl.ds(0, len(FAR))], b2.at[pl.ds(0, len(FAR))], recv_d.at[0]).wait()
+    await_far(recv_d)
 
     def deep_sweep(v, store, tier, first, padded, lo, hi):
         mid = v if padded else v[1:-1]
@@ -447,7 +526,7 @@
     for k in range(3):
         cells = {x2: coarse_rows(k, x2) for x2 in range(-2, 4)}
         up.append(jnp.stack([cells[x // 2] for x in range(-H, X1 + H)], axis=0))
-    arrive(copies_w)
+    arrive(NEAR, copies_w)
     held = inside(X1, H, R1, Y1) > 0.5
     v = [jnp.where(held, v2b[k], 0.0) + up[k] for k in range(3)]
     v = sweep(v, cs1[1], None, [co1[k] for k in range(3)], [first1[k] for k in range(3)], 2)
@@ -459,7 +538,7 @@
         pe1[k, :, pl.ds(1, Y1, stride=2), :] = v[k][:, :Y1]
         t = v[k][:, Y1:]
         pe1[k, :, Y0:R0, :] = jnp.where(row8 == 1, roll(t, 1, -2), jnp.where(row8 == 6, roll(t, -1, -2), t))
-    arrive(copies_v)
+    arrive(NEAR, copies_v)
     up = []
     held = co0[2] > 0.0
     for k in range(3):
@@ -471,8 +550,8 @@
     v = sweep(v, c_12[1:-1], None, inner, [first0[k, 2:-2, :Y0] for k in range(3)], 1, Y0)
     for k in range(3):
         out[k] = v[k]
-    leave(copies_w)
-    pltpu.make_async_copy(b2.at[pl.ds(0, len(FAR))], b2.at[pl.ds(0, len(FAR))], send_d.at[0]).wait()
+    leave(NEAR, copies_w)
+    await_far(send_d)
 
 
 def cycle(forces, modulus, occupancy, bonded):
@@ -507,9 +586,9 @@
             vmem((3, 6, R0, 128), F32),
             dma((4,)),
             dma((8,)), dma((8,)), dma((8,)), dma((8,)), dma((8,)), dma((8,)), dma((8,)), dma((8,)), dma((8,)), dma((8,)),
-            dma((len(COLUMN),)), dma((len(COLUMN),)), dma((len(ROW),)), dma((len(ROW),)), dma((1,)), dma((1,)),
+            dma((len(COLUMN),)), dma((len(COLUMN),)), dma((len(ROW),)), dma((len(ROW),)), dma((GB,)), dma((GB,)),
         ],
-        compiler_params=pltpu.CompilerParams(collective_id=0, has_side_effects=True, vmem_limit_bytes=48 << 20),
+        compiler_params=pltpu.CompilerParams(collective_id=0, has_side_effects=True, vmem_limit_bytes=56 << 20),
     )(forces, modulus, occupancy, bonded)
 
 

time: 56.6 us -> 42.5 us (0.75)
  Pallas kernels: 52.2 us -> 40.2 us
  local copies, waits for them, and re-layouts: 4.12 us -> 1.62 us
    pallas_call x1, Pallas kernels: 52.2 us -> 40.2 us  [cycle(): pl.pallas_call(body, out_shape=jax.ShapeDtypeStruct((3, X0, Y0, 128), F32...]
    unnamed x9 -> x1, local copies, waits for them, and re-layouts: 4.12 us -> 1.62 us
where the time goes in v2:
time: 42.5 us; the launch traced here: 41.8 us
  Pallas kernels  40.2 us (95%)
  local copies, waits for them, and re-layouts  1.62 us (4%)
    pallas_call x1, Pallas kernels, cycle(): pl.pallas_call(body, out_shape=jax.ShapeDtypeStruct((3, X0, Y0, 128), F32...  40.2 us
    unnamed x1, local copies, waits for them, and re-layouts  1.62 us

profile of v2, /device:TPU:1, one launch (start us, length us, event | category | flops | bytes accessed | tf_op | source)
XLA Modules:
  0.0 41.8 jit_solution(16182268837889068071)
XLA Ops:
  0.0 40.2 %shard_map.46 = f32[3,8,16,128]{3,2,1,0:T(8,128)} custom-call(f32[3,8,16,128]{3,2,1,0:T(8,128)} %forces.1, f32[8,16,128]{2,1,0:T(8,128)} %modulus.1, s32[8,16,128]{2,1,0:T(8,128)} %occupancy.1, s32[8,16,128]{2,1,0:T(8,128)} %bonded.1), custom_call_target="tpu_custom_call" | custom-call | tf_op jit(solution)/shard_map/pallas_call | solution.py:560
  40.2 1.6 %copy.6 = f32[3,8,16,128]{3,2,1,0:T(8,128)} copy(f32[3,8,16,128]{3,2,1,0:T(8,128)} %shard_map.46) | data formatting | bytes 393216

commit v3 on v2

--- a/solution.py
+++ b/solution.py
@@ -148,13 +148,18 @@
 def body(
     forces, modulus, occupancy, bonded, out, raw, mod_v, occ_v, bon_v, cs1, b1, v2a, v2b, first0, first1, co0, co1,
     pair, cs2, b2, sent2, co2, co3, e2, pe2, pe1,
-    load_sem, send_a, recv_a, send_b, recv_b, send_k, recv_k, send_v, recv_v, send_w, recv_w,
+    load_sem, send_c, recv_c, send_a, recv_a, send_b, recv_b, send_k, recv_k, send_v, recv_v, send_w, recv_w,
     send_g, recv_g, send_h, recv_h, send_d, recv_d,
 ):
     me_l, me_b = lax.axis_index("len"), lax.axis_index("brick")
 
     def device(dl, db):
-        return (lax.rem(me_l + dl + NL, NL), lax.rem(me_b + db + NB, NB))
+        at = me_l + dl
+        if dl > 0:
+            at = jnp.where(at >= NL, at - NL, at)
+        elif dl < 0:
+            at = jnp.where(at < 0, at + NL, at)
+        return (at, me_b + db)
 
     loads = [
         pltpu.make_async_copy(modulus, mod_v, load_sem.at[0]),
@@ -162,8 +167,6 @@
         pltpu.make_async_copy(bonded, bon_v, load_sem.at[2]),
         pltpu.make_async_copy(forces, raw.at[pl.ds(0, 3), pl.ds(H, X0), pl.ds(0, Y0), :], load_sem.at[3]),
     ]
-    for load in loads:
-        load.start()
     def exists(db):
         return jnp.logical_and(me_b + db >= 0, me_b + db < NB)
 
@@ -187,6 +190,8 @@
                 pl.semaphore_signal(barrier, inc=1, device_id=device(dl, db), device_id_type=MESH)
 
         where_exists(db, greet)
+    for load in loads:
+        load.start()
 
     def start(pairs, copies):
         for db, group in by_brick(pairs):
@@ -215,7 +220,8 @@
 
             where_exists(db, done)
 
-    def exchange(buf, sends, recvs, width, size_x, size_y, rows, off):
+    def exchange(buf, sends, recvs, width, size_x, size_y, rows, off, low=0, count=None):
+        fields = pl.ds(low, buf.shape[0] if count is None else count)
         copies = []
         for i, (dl, db) in enumerate(NEAR):
             xs, xd, nx = {
@@ -230,8 +236,8 @@
             }[db]
             copies.append(
                 pltpu.make_async_remote_copy(
-                    src_ref=buf.at[:, pl.ds(xs, nx), pl.ds(ys, ny), :],
-                    dst_ref=buf.at[:, pl.ds(xd, nx), pl.ds(yd, ny), :],
+                    src_ref=buf.at[fields, pl.ds(xs, nx), pl.ds(ys, ny), :],
+                    dst_ref=buf.at[fields, pl.ds(xd, nx), pl.ds(yd, ny), :],
                     send_sem=sends.at[i],
                     recv_sem=recvs.at[i],
                     device_id=device(dl, db),
@@ -277,7 +283,8 @@
     for db, group in by_brick(GREETED):
         greeters = greeters + (len(group) if db == 0 else len(group) * exists(db).astype(jnp.int32))
     pl.semaphore_wait(barrier, greeters)
-    copies_a = exchange(raw, send_a, recv_a, H, X0, Y0, R0, H)
+    copies_c = exchange(raw, send_c, recv_c, H, X0, Y0, R0, H, 4, 1)
+    copies_a = exchange(raw, send_a, recv_a, 2, X0, Y0, R0, H, 0, 4)
     clear(raw, R0, Y0)
     clear(cs1, R1, Y1)
     clear(b1, R1, Y1)
@@ -353,6 +360,8 @@
         store[4] = e
         buf[n_f - 1] = c
 
+    arrive(NEAR, copies_c)
+    leave(NEAR, copies_c)
     arrive(NEAR, copies_a)
     leave(NEAR, copies_a)
     coefficients(raw, co0, X0, R0, Y0, 1)
@@ -414,8 +423,8 @@
         def spread(db=db, group=group):
             for _, dl in group:
                 pltpu.make_async_remote_copy(
-                    src_ref=sent2,
-                    dst_ref=b2.at[pl.ds((DEEP - db) * NL + me_l, 1)],
+                    src_ref=sent2.at[:, pl.ds(0, 6)],
+                    dst_ref=b2.at[pl.ds((DEEP - db) * NL + me_l, 1), pl.ds(0, 6)],
                     send_sem=send_d.at[DEEP + db],
                     recv_sem=recv_d.at[DEEP - db],
                     device_id=device(dl, db),
@@ -428,7 +437,7 @@
         for db, group in by_brick(FAR):
 
             def done(db=db, count=len(group)):
-                held = b2.at[pl.ds(0, count)]
+                held = b2.at[pl.ds(0, count), pl.ds(0, 6)]
                 pltpu.make_async_copy(held, held, sems.at[DEEP + db]).wait()
 
             where_exists(db, done)
@@ -470,6 +479,9 @@
     c3 = COARSE_SCALE * restrict_deep(c2[1:-1])
     deep_coefficients(c3, smooth_deep(c3, 3, True), restrict_deep(s2), co3)
 
+    leave(NEAR, copies_w)
+    await_far(send_d)
+    arrive(NEAR, copies_v)
     await_far(recv_d)
 
     def deep_sweep(v, store, tier, first, padded, lo, hi):
@@ -483,7 +495,7 @@
             + store[2, lo:hi] * smooth_deep(c * v, tier, padded)
         )
 
-    source = b2[...].reshape(GB, NL, 8, 128)
+    source = jnp.where(row8 < 6, b2[...], 0.0).reshape(GB, NL, 8, 128)
     v1 = co2[2] * source
     v2 = deep_sweep(v1, co2, 2, v1, True, 0, GB)
     c = co2[3]
@@ -538,7 +550,6 @@
         pe1[k, :, pl.ds(1, Y1, stride=2), :] = v[k][:, :Y1]
         t = v[k][:, Y1:]
         pe1[k, :, Y0:R0, :] = jnp.where(row8 == 1, roll(t, 1, -2), jnp.where(row8 == 6, roll(t, -1, -2), t))
-    arrive(NEAR, copies_v)
     up = []
     held = co0[2] > 0.0
     for k in range(3):
@@ -550,8 +561,6 @@
     v = sweep(v, c_12[1:-1], None, inner, [first0[k, 2:-2, :Y0] for k in range(3)], 1, Y0)
     for k in range(3):
         out[k] = v[k]
-    leave(NEAR, copies_w)
-    await_far(send_d)
 
 
 def cycle(forces, modulus, occupancy, bonded):
@@ -586,6 +595,7 @@
             vmem((3, 6, R0, 128), F32),
             dma((4,)),
             dma((8,)), dma((8,)), dma((8,)), dma((8,)), dma((8,)), dma((8,)), dma((8,)), dma((8,)), dma((8,)), dma((8,)),
+            dma((8,)), dma((8,)),
             dma((len(COLUMN),)), dma((len(COLUMN),)), dma((len(ROW),)), dma((len(ROW),)), dma((GB,)), dma((GB,)),
         ],
         compiler_params=pltpu.CompilerParams(collective_id=0, has_side_effects=True, vmem_limit_bytes=56 << 20),

time: 42.5 us -> 40.7 us (0.958)
  Pallas kernels: 40.2 us -> 38.8 us
    pallas_call x1, Pallas kernels: 40.2 us -> 38.8 us  [cycle(): pl.pallas_call(body, out_shape=jax.ShapeDtypeStruct((3, X0, Y0, 128), F32...]
where the time goes in v3:
time: 40.7 us; the launch traced here: 40.5 us
  Pallas kernels  38.8 us (95%)
  local copies, waits for them, and re-layouts  1.62 us (4%)
    pallas_call x1, Pallas kernels, cycle(): pl.pallas_call(body, out_shape=jax.ShapeDtypeStruct((3, X0, Y0, 128), F32...  38.8 us
    unnamed x1, local copies, waits for them, and re-layouts  1.62 us

profile of v3, /device:TPU:1, one launch (start us, length us, event | category | flops | bytes accessed | tf_op | source)
XLA Modules:
  0.0 40.5 jit_solution(15078556784236880139)
XLA Ops:
  0.0 38.8 %shard_map.46 = f32[3,8,16,128]{3,2,1,0:T(8,128)} custom-call(f32[3,8,16,128]{3,2,1,0:T(8,128)} %forces.1, f32[8,16,128]{2,1,0:T(8,128)} %modulus.1, s32[8,16,128]{2,1,0:T(8,128)} %occupancy.1, s32[8,16,128]{2,1,0:T(8,128)} %bonded.1), custom_call_target="tpu_custom_call" | custom-call | tf_op jit(solution)/shard_map/pallas_call | solution.py:569
  38.8 1.6 %copy.6 = f32[3,8,16,128]{3,2,1,0:T(8,128)} copy(f32[3,8,16,128]{3,2,1,0:T(8,128)} %shard_map.46) | data formatting | bytes 393216
